TPU v7x, 512 devices: a whole 4x8x8 slice. The times are simulated.
512 devices in a mesh: wide: 64 (over x, y, core), row: 8 (over z).
Axes of the slice: x: 4, y: 8, z: 8, core: 2. Of those that a mesh axis runs over, the one named last changes fastest.
Arguments:
- points: float32 [128, 65536], P(None, ('wide', 'row')), may hold values from -6 to 6
- targets: float32 [32, 65536], P(None, ('wide', 'row')), may hold values from -6 to 6
- lengthscales: float32 [128], replicated, may hold values from 3.5 to 7
- outputscale: float32 [1], replicated, may hold values from 0.5 to 2
- noise: float32 [1], replicated, may hold values from 0.5 to 2
Outputs:
- solution: float32 [32, 65536], P(None, ('wide', 'row'))
- residual: float32 [32, 65536], P(None, ('wide', 'row'))
All inputs are finite; a program needn't handle non-finite values.
Results may differ from a plain program's by a relative error of at most 0.0003.
Values sent between devices are 32-bit elements; how exact they have to be, the bound alone decides.
No kernel may reach another device: no remote copies, remote signals or barrier semaphores. Data moves between devices by JAX's collectives and lax.ppermute only.
A program may use at most 64 MiB of HBM per device.

v0:
```python
import functools
import math

import jax
import jax.numpy as jnp
from jax import lax
from jax.experimental import pallas as pl
from jax.experimental.pallas import tpu as pltpu
from jax.sharding import Mesh
from jax.sharding import PartitionSpec as P


AXES = ("x", "y", "c", "z")
F32 = jnp.float32
BF16 = jnp.bfloat16
ROOT = math.sqrt(math.log2(math.e))
BLK = 128
RHS = 32
TILE = 512
SUB = 256
WIDE = 1024
VMEM = pl.BlockSpec(memory_space=pltpu.VMEM)
SMEM = pl.BlockSpec(memory_space=pltpu.SMEM)
PARAMS = pltpu.CompilerParams(vmem_limit_bytes=12 << 20)


def shift(value, axis, steps):
    count = lax.axis_size(axis)
    return lax.ppermute(value, axis, [(s, (s + steps) % count) for s in range(count)])


def exchange(x, axes):
    return lax.all_to_all(x, axes, 0, 0, tiled=True)


def halves(x):
    high = x.astype(BF16)
    return high, (x - high.astype(F32)).astype(BF16)


def kept(x):
    return pltpu.with_memory_space_constraint(x, pltpu.VMEM)


def cost(flops=0, moved=0, powers=0):
    return pl.CostEstimate(flops=flops, bytes_accessed=moved, transcendentals=powers)


def spread_kernel(points_in, lengths_in, targets_in, scale, noise, out, own, aux, points, lengths, targets, sems):
    copies = [
        pltpu.make_async_copy(source, to, sems.at[at])
        for at, (source, to) in enumerate(((points_in, points), (lengths_in, lengths), (targets_in, targets)))
    ]
    for copy in copies:
        copy.start()
    for copy in copies:
        copy.wait()
    scaled = points[...] / jnp.broadcast_to(lengths[...], (BLK, BLK)).T
    vectors = targets[...]
    own[...] = scaled
    for peer in range(8):
        out[peer, pl.ds(0, BLK), :] = scaled
        out[peer, pl.ds(BLK, RHS), :] = vectors
    aux[...] = jnp.where(lax.broadcasted_iota(jnp.int32, (8, BLK), 0) == 0, scale[0], noise[0])


def spread(points, lengths, targets, scale, noise):
    return pl.pallas_call(
        spread_kernel,
        in_specs=[pl.BlockSpec(memory_space=pltpu.HBM)] * 3 + [SMEM, SMEM],
        out_specs=[VMEM] * 3,
        scratch_shapes=[
            pltpu.VMEM((BLK, BLK), F32),
            pltpu.VMEM((1, BLK), F32),
            pltpu.VMEM((RHS, BLK), F32),
            pltpu.SemaphoreType.DMA((3,)),
        ],
        out_shape=[
            jax.ShapeDtypeStruct((8, BLK + RHS, BLK), F32),
            jax.ShapeDtypeStruct((BLK, BLK), F32),
            jax.ShapeDtypeStruct((8, BLK), F32),
        ],
        compiler_params=PARAMS,
        name="spread",
    )(*[pltpu.with_memory_space_constraint(v, pltpu.HBM) for v in (points, lengths, targets)], scale, noise)


ORDER = (0, -1, 1, 4, -3, -2, 2, 3)


def prepare_rows(values, left, left_sq):
    for block, value in enumerate(values):
        value = value * ROOT
        high, low = halves(value)
        at, lanes = block * BLK // TILE, pl.ds(block * BLK % TILE, BLK)
        left[at, pl.ds(0, 128), lanes] = high
        left[at, pl.ds(128, 128), lanes] = low
        left[at, pl.ds(256, 128), lanes] = high
        left[at, pl.ds(384, 128), lanes] = low
        left_sq[at, :, lanes] = -0.5 * jnp.sum(value * value, axis=0, keepdims=True)


def place_of(tile, local):
    return lax.rem(lax.axis_index("z") + (ORDER[tile % 2 * 4 + local] + 8), 8)


def prepare_cols(col_refs, right, right_sq, vecs):
    each = 8 // len(col_refs)
    for block in range(8):
        ref, at = col_refs[block // each], block % each
        value = ref[at, pl.ds(0, BLK), :].T * ROOT
        high, low = halves(value)
        rows = pl.ds(block * BLK, BLK)
        right[rows, pl.ds(0, 128)] = high
        right[rows, pl.ds(128, 128)] = high
        right[rows, pl.ds(256, 128)] = low
        right[rows, pl.ds(384, 128)] = low
        right_sq[rows, :] = -0.5 * jnp.sum(value * value, axis=1, keepdims=True)
        high, low = halves(ref[at, pl.ds(BLK, RHS), :])
        vecs[pl.ds(0, RHS), rows] = high
        vecs[pl.ds(RHS, RHS), rows] = low


def make_values(left, left_sq, right, right_sq, vecs, high, low):
    for step in range(WIDE // SUB):
        rows = pl.ds(step * SUB, SUB)
        power = jnp.dot(right[rows, :], left[...], preferred_element_type=F32)
        high[rows, :], low[rows, :] = halves(jnp.exp2(power + right_sq[rows, :] + left_sq[...]))
    both = jnp.dot(vecs[...], high[...], preferred_element_type=F32)
    rest = jnp.dot(vecs[pl.ds(0, RHS), :], low[...], preferred_element_type=F32)
    product = both[:RHS] + both[RHS:] + rest
    return [product[:, local * BLK : (local + 1) * BLK] for local in range(TILE // BLK)]


def cols_kernel(cols, right, right_sq, vecs):
    prepare_cols((cols,), right, right_sq, vecs)


def own_kernel(count, *refs):
    blocks, (right, right_sq, vecs, out, high, low, left, left_sq) = refs[:count], refs[count:]
    values = []
    for ref in blocks:
        values += [ref[...]] if len(ref.shape) == 2 else [ref[at] for at in range(ref.shape[0])]
    prepare_rows(values, left, left_sq)
    for to in range(len(values) * BLK // TILE):
        made = make_values(left.at[to], left_sq.at[to], right, right_sq, vecs, high.at[to], low.at[to])
        for local, piece in enumerate(made):
            out[to * 4 + local] = piece


def more_kernel(tiles, last, *refs):
    cols, refs = refs[:2], refs[2:]
    lefts, befores, (out, high, low, right, right_sq, vecs) = refs[:6], refs[6:-6], refs[-6:]
    prepare_cols(cols, right, right_sq, vecs)
    for to, tile in enumerate(tiles):
        ref, at = WHERE[tile]
        made = make_values(
            lefts[ref].at[at], lefts[3 + ref].at[at], right, right_sq, vecs, high.at[to], low.at[to]
        )
        for local, piece in enumerate(made):
            before = befores[0][tile * 4 + local] if len(befores) == 1 else befores[ref][at * 4 + local]
            out[place_of(tile, local) if last else to * 4 + local] = piece + before


WHERE = ((0, 0), (1, 0), (2, 0), (2, 1))
ALL, MINE, THEIRS = (0, 1, 2, 3), (0, 1), (2, 3)


def made(tiles):
    values = pltpu.VMEM((len(tiles), WIDE, TILE), BF16)
    return [pltpu.VMEM((len(tiles) * TILE // BLK, RHS, BLK), F32), values, values]


def made_cost(tiles):
    width = len(tiles) * TILE
    return cost(2 * width * WIDE * 768, 4 * width * WIDE, width * WIDE)


RIGHT = [pltpu.VMEM((WIDE, 512), BF16), pltpu.VMEM((WIDE, 1), F32), pltpu.VMEM((2 * RHS, WIDE), BF16)]


def own_cols(cols):
    return pl.pallas_call(
        cols_kernel,
        in_specs=[VMEM],
        out_specs=[VMEM] * 3,
        out_shape=RIGHT,
        compiler_params=PARAMS,
        cost_estimate=cost(0, 2 << 20, 0),
        name="own_cols",
    )(cols)


def own_chunk(blocks, cols, tiles):
    return pl.pallas_call(
        functools.partial(own_kernel, len(blocks)),
        in_specs=[VMEM] * (len(blocks) + 3),
        out_specs=[VMEM] * 5,
        out_shape=[*made(tiles), pltpu.VMEM((len(tiles), 512, TILE), BF16), pltpu.VMEM((len(tiles), 1, TILE), F32)],
        compiler_params=PARAMS,
        cost_estimate=made_cost(tiles),
    )(*blocks, *[kept(v) for v in cols])


def more_chunk(tiles, cols, lefts, befores, last=False):
    return pl.pallas_call(
        functools.partial(more_kernel, tiles, last),
        in_specs=[VMEM] * (8 + len(befores)),
        out_specs=[VMEM] * 3,
        out_shape=made(tiles),
        scratch_shapes=RIGHT,
        compiler_params=PARAMS,
        cost_estimate=made_cost(tiles),
    )(*cols, *[kept(v) for v in lefts], *[kept(v) for v in befores])


def total(x):
    return jnp.sum(x, axis=1, keepdims=True)


def between_kernel(aux, arrived, targets, first_ref, wide_ref):
    first = aux[0:1, 0:1] * jnp.sum(arrived[...], axis=0) + aux[1:2, 0:1] * targets[...]
    first_ref[...] = first
    for peer in range(32):
        wide_ref[peer] = first


def between(aux, arrived, targets):
    return pl.pallas_call(
        between_kernel,
        in_specs=[VMEM] * 3,
        out_specs=[VMEM] * 2,
        out_shape=[jax.ShapeDtypeStruct((RHS, BLK), F32), jax.ShapeDtypeStruct((32, RHS, BLK), F32)],
        compiler_params=PARAMS,
        name="between",
    )(aux, arrived, targets)


def second_kernel(tiles, gathered, *refs):
    highs, lows, out, vecs = refs[0:7], refs[7:14], refs[14], refs[15]
    place = lax.axis_index("x")
    for chunk in range(4):
        source = lax.rem(place + (0, 3, 1, 2)[chunk], 4) * 8
        for y in range(8):
            lanes = pl.ds(y * BLK, BLK)
            high, low = halves(gathered[source + y])
            vecs[chunk, pl.ds(0, RHS), lanes] = high
            vecs[chunk, pl.ds(RHS, RHS), lanes] = low
    for tile in tiles:
        product = jnp.zeros((RHS, TILE), F32)
        for chunk in range(4):
            ref, at = ((0, 1, 2, 2)[tile], (0, 0, 0, 1)[tile]) if chunk == 0 else (2 + chunk, tile)
            if chunk == 3:
                ref, at = 5 + tile // 2, tile % 2
            both = jnp.dot(vecs[chunk], highs[ref][at], preferred_element_type=F32)
            rest = jnp.dot(vecs[chunk, pl.ds(0, RHS), :], lows[ref][at], preferred_element_type=F32)
            product = product + both[:RHS] + both[RHS:] + rest
        for local in range(TILE // BLK):
            out[place_of(tile, local)] = product[:, local * BLK : (local + 1) * BLK]


def second(tiles, gathered, highs, lows):
    width = len(tiles) * TILE
    return pl.pallas_call(
        functools.partial(second_kernel, tiles),
        in_specs=[VMEM] * (1 + len(highs) + len(lows)),
        out_specs=VMEM,
        out_shape=pltpu.VMEM((width // BLK, RHS, BLK), F32),
        scratch_shapes=[pltpu.VMEM((4, 2 * RHS, WIDE), BF16)],
        compiler_params=PARAMS,
        cost_estimate=cost(2 * width * 4 * WIDE * 128, 4 * width * 4 * WIDE, 0),
    )(gathered, *[kept(v) for v in highs], *[kept(v) for v in lows])


def total(x):
    return jnp.sum(x, axis=1, keepdims=True)


def settle_kernel(aux, arrived, targets, first_ref, second_ref, dots_ref):
    vectors, first = targets[...], first_ref[...]
    second_image = aux[0:1, 0:1] * jnp.sum(arrived[...], axis=0) + aux[1:2, 0:1] * first
    second_ref[...] = second_image
    dots = (vectors * vectors, vectors * first, first * first, first * second_image)
    lane = lax.broadcasted_iota(jnp.int32, (RHS, BLK), 1)
    wide = jnp.zeros((RHS, BLK), F32)
    for at, dot in enumerate(dots):
        wide = jnp.where(lane == at, total(dot), wide)
    tall = jnp.concatenate([wide, jnp.zeros((BLK - RHS, BLK), F32)], axis=0).T
    row = tall[0:1]
    for at in range(1, 4):
        row = row + pltpu.roll(tall[at : at + 1], at * RHS, 1)
    dots_ref[...] = jnp.broadcast_to(row, (8, BLK))


def settle(aux, arrived, targets, first):
    return pl.pallas_call(
        settle_kernel,
        in_specs=[VMEM] * 4,
        out_specs=[VMEM] * 2,
        out_shape=[jax.ShapeDtypeStruct((RHS, BLK), F32), jax.ShapeDtypeStruct((8, BLK), F32)],
        compiler_params=PARAMS,
        name="settle",
    )(aux, arrived, targets, first)


def finish_kernel(sums, targets, first_ref, second_ref, solution_ref, residual_ref):
    row = jnp.broadcast_to(jnp.sum(sums[...], axis=0), (8, BLK))
    sub = lax.broadcasted_iota(jnp.int32, (8, BLK), 0)
    rows = jnp.zeros((8, BLK), F32)
    for at in range(4):
        rows = jnp.where(sub == at, pltpu.roll(row, (BLK - at * RHS) % BLK, 1), rows)
    tall = jnp.concatenate([rows, jnp.zeros((BLK - 8, BLK), F32)], axis=0).T
    norm, curve, square, cubic = [tall[:RHS, at : at + 1] for at in range(4)]
    vectors, first = targets[...], first_ref[...]
    step = norm / curve
    norm_next = norm - 2.0 * step * curve + step * step * square
    more = 1.0 + norm_next / norm
    new_curve = more * more * curve - 2.0 * step * more * square + step * step * cubic
    new_step = norm_next / new_curve
    solution_ref[...] = step * vectors + new_step * (more * vectors - step * first)
    residual_ref[...] = vectors - step * first - new_step * (more * first - step * second_ref[...])


def finish(sums, targets, first, second_image):
    shape = jax.ShapeDtypeStruct((RHS, BLK), F32)
    return pl.pallas_call(
        finish_kernel,
        in_specs=[VMEM] * 4,
        out_specs=[VMEM] * 2,
        out_shape=[shape, shape],
        compiler_params=PARAMS,
        name="finish",
    )(sums, targets, first, second_image)


def to_each(x, axes):
    peers = lax.axis_size(axes)
    return exchange(jnp.broadcast_to(x[None], (peers, *x.shape)), axes)


def on_device(points, targets, lengthscales, outputscale, noise):
    near, own, aux = spread(points, lengthscales[None], targets, outputscale, noise)
    near = exchange(near, "y")
    behind_low, ahead_high = shift(near[:4], "x", 1), shift(near[4:], "x", -1)
    behind_high, ahead_low = shift(near[4:], "x", 1), shift(near[:4], "x", -1)
    across = [shift(behind_low, "x", 1), shift(ahead_high, "x", -1)]
    below, above, far = shift(own, "z", 1), shift(own, "z", -1), shift(own, "z", 4)
    pairs = [shift(jnp.stack([below, own]), "z", 2), shift(jnp.stack([own, above]), "z", -2)]
    prepared = own_cols(near)
    chunks = []
    chunks.append(own_chunk([own, below, above, far], prepared, (0,)))
    same = jnp.concatenate([jnp.stack([own, below, above, far]), *pairs])
    other = shift(same, "c", 1)
    chunks.append(own_chunk(pairs, prepared, (1,)))
    chunks.append(own_chunk([other], prepared, THEIRS))
    pieces, highs, lows, left, left_sq = [list(part) for part in zip(*chunks)]
    lefts = [*left, *left_sq]
    for cols in ([behind_low, behind_high], [ahead_low, ahead_high]):
        piece, high, low = more_chunk(ALL, cols, lefts, pieces)
        pieces = [piece]
        highs.append(high)
        lows.append(low)
    theirs, high_theirs, low_theirs = more_chunk(THEIRS, across, lefts, pieces, True)
    theirs = shift(theirs, "c", 1)
    mine, high_mine, low_mine = more_chunk(MINE, across, lefts, pieces, True)
    highs += [high_mine, high_theirs]
    lows += [low_mine, low_theirs]
    arrived = exchange(mine + theirs, "z")
    first, wide = between(aux, arrived, targets)
    gathered = exchange(wide, ("x", "y"))
    theirs = shift(second(THEIRS, gathered, highs, lows), "c", 1)
    mine = second(MINE, gathered, highs, lows)
    arrived = exchange(mine + theirs, "z")
    second_image, dots = settle(aux, arrived, targets, first)
    sums = jnp.sum(to_each(dots[0:1], ("y", "c")), axis=0)
    return tuple(finish(to_each(sums, ("x", "z")), targets, first, second_image))


def solution(mesh):
    finer = Mesh(mesh.devices.reshape(4, 8, 2, mesh.shape["row"]), AXES)
    spec = P(None, AXES)

    return jax.shard_map(
        on_device, mesh=finer, in_specs=(spec, spec, P(), P(), P()), out_specs=(spec, spec), check_vma=False
    )
```

profile of v0, /device:TPU:1, one launch (start us, length us, event | category | flops | bytes accessed | tf_op | source)
XLA Modules:
  0.0 172.6 jit_solution(12686965648915555699)
XLA Ops:
  1.9 1.8 %spread.1 = (f32[8,160,128]{2,1,0:T(8,128)}, f32[128,128]{1,0:T(8,128)S(1)}, f32[8,128]{1,0:T(8,128)S(1)}) custom-call(f32[128,128]{1,0:T(8,128)} %points_in.1, f32[1,128]{1,0:T(1,128)} %bitcast.16, f32[32,128]{1,0:T(8,128)} %targets.5, f32[1]{0:T(128)S(6)} %copy.13.scale, f32[1]{0:T(128)S(6)} %copy.14.noise), custom_call_target="tpu_custom_call" | custom-call | tf_op jit(solution)/shard_map/spread/pallas_call | solution.py:68
  3.8 11.5 %collective-permute-start.6 = (f32[128,128]{1,0:T(8,128)S(1)}, f32[128,128]{1,0:T(8,128)S(1)}, u32[]{:S(2)}, u32[]{:S(2)}) collective-permute-start(f32[128,128]{1,0:T(8,128)S(1)} %get-tuple-element.41.refs_0_), channel_id=1, source_target_pairs={{0,4},{1,5},{2,6},{3,7},{4,0},{5,1},{6,2},{7,3},{8,12},{9,13},{10,... | collective-permute-start | bytes 196616 | tf_op jit(solution)/shard_map/ppermute | solution.py:29
  15.2 2.0 %collective-permute-start.5 = (f32[128,128]{1,0:T(8,128)S(1)}, f32[128,128]{1,0:T(8,128)S(1)}, u32[]{:S(2)}, u32[]{:S(2)}) collective-permute-start(f32[128,128]{1,0:T(8,128)S(1)} %get-tuple-element.41.refs_0_), channel_id=1, source_target_pairs={{0,7},{1,0},{2,1},{3,2},{4,3},{5,4},{6,5},{7,6},{8,15},{9,8},{10,9... | collective-permute-start | bytes 196616 | tf_op jit(solution)/shard_map/ppermute | solution.py:29
  17.2 3.3 %collective-permute-start.4 = (f32[128,128]{1,0:T(8,128)S(1)}, f32[128,128]{1,0:T(8,128)S(1)}, u32[]{:S(2)}, u32[]{:S(2)}) collective-permute-start(f32[128,128]{1,0:T(8,128)S(1)} %get-tuple-element.41.refs_0_), channel_id=1, source_target_pairs={{0,1},{1,2},{2,3},{3,4},{4,5},{5,6},{6,7},{7,0},{8,9},{9,10},{10,1... | collective-permute-start | bytes 196616 | tf_op jit(solution)/shard_map/ppermute | solution.py:29
  20.5 6.8 %all-to-all-start = ((f32[8,160,128]{2,1,0:T(8,128)}), f32[8,160,128]{2,1,0:T(8,128)S(1)}, u32[]{:S(2)}, u32[]{:S(2)}) async-start(f32[8,160,128]{2,1,0:T(8,128)} %get-tuple-element.40), calls=%async_computation | async-start | bytes 1310720 | tf_op jit(solution)/shard_map/all_to_all | solution.py:33
  27.4 0.0 collective-permute-done.5.refs_2_
  27.4 0.0 collective-permute-done.4.refs_1_
  27.4 1.9 %collective-permute-start.8 = (f32[2,128,128]{2,1,0:T(8,128)S(1)}, f32[2,128,128]{2,1,0:T(8,128)S(1)}, u32[]{:S(2)}, u32[]{:S(2)}) collective-permute-start(f32[2,128,128]{2,1,0:T(8,128)S(1)} %get-tuple-element.78), channel_id=1, source_target_pairs={{0,6},{1,7},{2,0},{3,1},{4,2},{5,3},{6,4},{7,5},{8,14},{9,15},{10,... | collective-permute-start | bytes 393224 | tf_op jit(solution)/shard_map/ppermute | solution.py:29
  29.4 4.2 %collective-permute-start.7 = (f32[2,128,128]{2,1,0:T(8,128)S(1)}, f32[2,128,128]{2,1,0:T(8,128)S(1)}, u32[]{:S(2)}, u32[]{:S(2)}) collective-permute-start(f32[2,128,128]{2,1,0:T(8,128)S(1)} %get-tuple-element.79), channel_id=1, source_target_pairs={{0,2},{1,3},{2,4},{3,5},{4,6},{5,7},{6,0},{7,1},{8,10},{9,11},{10,... | collective-permute-start | bytes 393224 | tf_op jit(solution)/shard_map/ppermute | solution.py:29
  33.6 0.0 collective-permute-done.6.refs_3_
  33.7 4.5 %collective-permute-done.7.refs_0_ = f32[2,128,128]{2,1,0:T(8,128)S(1)} collective-permute-done((f32[2,128,128]{2,1,0:T(8,128)S(1)}, f32[2,128,128]{2,1,0:T(8,128)S(1)}, u32[]{:S(2)}, u32[]{:S(2)}) %collective-permute-start.7) | collective-permute-done | bytes 131104 | tf_op jit(solution)/shard_map/ppermute | solution.py:29
  38.1 0.0 collective-permute-done.8.refs_1_
  38.2 4.4 %collective-permute-start.9 = (f32[8,128,128]{2,1,0:T(8,128)S(1)}, f32[8,128,128]{2,1,0:T(8,128)S(1)}, u32[]{:S(2)}, u32[]{:S(2)}) collective-permute-start(f32[8,128,128]{2,1,0:T(8,128)S(1)} %constant_dynamic-update-slice_fusion), channel_id=1, source_target_pairs={{0,8},{8,0},{1,9},{9,1},{2,10},{10,2},{3,11},{11,3},{4,12},{12,4},... | collective-permute-start | bytes 1572872 | tf_op jit(solution)/shard_map/ppermute | solution.py:29
  42.6 4.1 %all-to-all-done.cols = f32[8,160,128]{2,1,0:T(8,128)S(1)} async-done(((f32[8,160,128]{2,1,0:T(8,128)}), f32[8,160,128]{2,1,0:T(8,128)S(1)}, u32[]{:S(2)}, u32[]{:S(2)}) %all-to-all-start) | async-done | bytes 655392 | tf_op jit(solution)/shard_map/all_to_all | solution.py:33
  46.7 4.4 %collective-permute-start.2 = (f32[4,160,128]{2,1,0:T(8,128)S(1)}, f32[4,160,128]{2,1,0:T(8,128)S(1)}, u32[]{:S(2)}, u32[]{:S(2)}) collective-permute-start(f32[4,160,128]{2,1,0:T(8,128)S(1)} %get-tuple-element.76), channel_id=1, source_target_pairs={{0,384},{128,0},{256,128},{384,256},{1,385},{129,1},{257,129},{385... | collective-permute-start | bytes 983048 | tf_op jit(solution)/shard_map/ppermute | solution.py:29
  51.1 1.9 %collective-permute-start = (f32[4,160,128]{2,1,0:T(8,128)S(1)}, f32[4,160,128]{2,1,0:T(8,128)S(1)}, u32[]{:S(2)}, u32[]{:S(2)}) collective-permute-start(f32[4,160,128]{2,1,0:T(8,128)S(1)} %get-tuple-element.77), channel_id=1, source_target_pairs={{0,128},{128,256},{256,384},{384,0},{1,129},{129,257},{257,385},{3... | collective-permute-start | bytes 983048 | tf_op jit(solution)/shard_map/ppermute | solution.py:29
  53.0 2.1 %collective-permute-start.11 = (f32[4,160,128]{2,1,0:T(8,128)S(1)}, f32[4,160,128]{2,1,0:T(8,128)S(1)}, u32[]{:S(2)}, u32[]{:S(2)}) collective-permute-start(f32[4,160,128]{2,1,0:T(8,128)S(1)} %get-tuple-element.76), channel_id=1, source_target_pairs={{0,128},{128,256},{256,384},{384,0},{1,129},{129,257},{257,385},{3... | collective-permute-start | bytes 983048 | tf_op jit(solution)/shard_map/ppermute | solution.py:29
  55.1 4.4 %collective-permute-start.10 = (f32[4,160,128]{2,1,0:T(8,128)S(1)}, f32[4,160,128]{2,1,0:T(8,128)S(1)}, u32[]{:S(2)}, u32[]{:S(2)}) collective-permute-start(f32[4,160,128]{2,1,0:T(8,128)S(1)} %get-tuple-element.77), channel_id=1, source_target_pairs={{0,384},{128,0},{256,128},{384,256},{1,385},{129,1},{257,129},{385... | collective-permute-start | bytes 983048 | tf_op jit(solution)/shard_map/ppermute | solution.py:29
  59.5 0.4 own_cols.1
  59.9 1.2 shard_map.69
  61.1 0.0 collective-permute-done.9.refs_0_
  61.1 2.3 %shard_map.70 = (f32[8,32,128]{2,1,0:T(8,128)S(1)}, bf16[2,1024,512]{2,1,0:T(8,128)(2,1)S(1)}, bf16[2,1024,512]{2,1,0:T(8,128)(2,1)S(1)}, bf16[2,512,512]{2,1,0:T(8,128)(2,1)S(1)}, f32[2,1,512]{2,1,0:T(1,128)S(1)}) custom-call(f32[8,128,128]{2,1,0:T(8,128)S(1)} %collective-permute-done.9.refs_0_, ...), custom_call_target="tpu_custom_call" | custom-call | flops 1610612736 | bytes 4194304 | tf_op jit(solution)/shard_map/pallas_call | solution.py:195
  63.4 1.2 shard_map.68
  64.6 0.0 collective-permute-done.2.refs_1_
  64.6 3.4 %collective-permute-start.3 = (f32[4,160,128]{2,1,0:T(8,128)S(1)}, f32[4,160,128]{2,1,0:T(8,128)S(1)}, u32[]{:S(2)}, u32[]{:S(2)}) collective-permute-start(f32[4,160,128]{2,1,0:T(8,128)S(1)} %collective-permute-done.2.refs_1_), channel_id=1, source_target_pairs={{0,384},{128,0},{256,128},{384,256},{1,385},{129,1},{257,129},{385... | collective-permute-start | bytes 983048 | tf_op jit(solution)/shard_map/ppermute | solution.py:29
  68.0 0.0 collective-permute-done.refs_0_
  68.0 2.1 %collective-permute-start.1 = (f32[4,160,128]{2,1,0:T(8,128)S(1)}, f32[4,160,128]{2,1,0:T(8,128)S(1)}, u32[]{:S(2)}, u32[]{:S(2)}) collective-permute-start(f32[4,160,128]{2,1,0:T(8,128)S(1)} %collective-permute-done.refs_0_), channel_id=1, source_target_pairs={{0,128},{128,256},{256,384},{384,0},{1,129},{129,257},{257,385},{3... | collective-permute-start | bytes 983048 | tf_op jit(solution)/shard_map/ppermute | solution.py:29
  70.1 0.0 collective-permute-done.11.refs_1_
  70.1 4.4 %shard_map.71 = (f32[16,32,128]{2,1,0:T(8,128)S(1)}, bf16[4,1024,512]{2,1,0:T(8,128)(2,1)S(1)}, bf16[4,1024,512]{2,1,0:T(8,128)(2,1)S(1)}) custom-call(f32[4,160,128]{2,1,0:T(8,128)S(1)} %collective-permute-done.refs_0_, f32[4,160,128]{2,1,0:T(8,128)S(1)} %collective-permute-done.11.refs_1_, bf16[1,512,512]{2,1,0:T(8,128)(2,1)S(1)} %get-tuple-element.45.refs_2_, ...), custom_call_target="tpu_custom_call" | custom-call | flops 3221225472 | bytes 8388608 | tf_op jit(solution)/shard_map/pallas_call | solution.py:206
  74.5 0.0 collective-permute-done.10.refs_0_
  74.6 4.6 %shard_map.72 = (f32[16,32,128]{2,1,0:T(8,128)S(1)}, bf16[4,1024,512]{2,1,0:T(8,128)(2,1)S(1)}, bf16[4,1024,512]{2,1,0:T(8,128)(2,1)S(1)}) custom-call(f32[4,160,128]{2,1,0:T(8,128)S(1)} %collective-permute-done.10.refs_0_, f32[4,160,128]{2,1,0:T(8,128)S(1)} %collective-permute-done.2.refs_1_, bf16[1,512,512]{2,1,0:T(8,128)(2,1)S(1)} %get-tuple-element.45.refs_2_, ...), custom_call_target="tpu_custom_call" | custom-call | flops 3221225472 | bytes 8388608 | tf_op jit(solution)/shard_map/pallas_call | solution.py:206
  79.1 0.0 collective-permute-done.3.refs_1_
  79.1 0.0 collective-permute-done.1.refs_0_
  79.1 2.5 %shard_map.74 = (f32[8,32,128]{2,1,0:T(8,128)S(1)}, bf16[2,1024,512]{2,1,0:T(8,128)(2,1)S(1)}, bf16[2,1024,512]{2,1,0:T(8,128)(2,1)S(1)}) custom-call(f32[4,160,128]{2,1,0:T(8,128)S(1)} %collective-permute-done.1.refs_0_, f32[4,160,128]{2,1,0:T(8,128)S(1)} %collective-permute-done.3.refs_1_, bf16[1,512,512]{2,1,0:T(8,128)(2,1)S(1)} %get-tuple-element.45.refs_2_, ...), custom_call_target="tpu_custom_call" | custom-call | flops 1610612736 | bytes 4194304 | tf_op jit(solution)/shard_map/pallas_call | solution.py:206
  81.6 0.0 copy-start
  81.6 5.3 %collective-permute-start.12 = (f32[8,32,128]{2,1,0:T(8,128)S(1)}, f32[8,32,128]{2,1,0:T(8,128)S(1)}, u32[]{:S(2)}, u32[]{:S(2)}) collective-permute-start(f32[8,32,128]{2,1,0:T(8,128)S(1)} %get-tuple-element.57), channel_id=1, source_target_pairs={{0,8},{8,0},{1,9},{9,1},{2,10},{10,2},{3,11},{11,3},{4,12},{12,4},... | collective-permute-start | bytes 393224 | tf_op jit(solution)/shard_map/ppermute | solution.py:29
  86.9 2.5 %shard_map.73 = (f32[8,32,128]{2,1,0:T(8,128)S(1)}, bf16[2,1024,512]{2,1,0:T(8,128)(2,1)S(1)}, bf16[2,1024,512]{2,1,0:T(8,128)(2,1)S(1)}) custom-call(f32[4,160,128]{2,1,0:T(8,128)S(1)} %collective-permute-done.1.refs_0_, f32[4,160,128]{2,1,0:T(8,128)S(1)} %collective-permute-done.3.refs_1_, bf16[1,512,512]{2,1,0:T(8,128)(2,1)S(1)} %get-tuple-element.45.refs_2_, ...), custom_call_target="tpu_custom_call" | custom-call | flops 1610612736 | bytes 4194304 | tf_op jit(solution)/shard_map/pallas_call | solution.py:206
  89.4 0.0 collective-permute-done.12
  89.4 13.8 %all_to_all.30.arrived = f32[8,32,128]{2,1,0:T(8,128)S(1)} all-to-all(f32[8,32,128]{2,1,0:T(8,128)S(1)} %add.6), channel_id=1, replica_groups=mesh['x'=4,'y'=8,'c'=2,'z'=8] {'z'}, dimensions={0} | all-to-all | bytes 262144 | tf_op jit(solution)/shard_map/all_to_all | solution.py:33
  103.2 0.0 copy-done
  103.2 0.1 between.1
  103.3 19.9 %all_to_all.31.gathered = f32[32,32,128]{2,1,0:T(8,128)S(1)} all-to-all(f32[32,32,128]{2,1,0:T(8,128)S(1)} %get-tuple-element.58), channel_id=1, replica_groups=mesh['x'=4,'y'=8,'c'=2,'z'=8] {'x','y'}, dimensions={0} | all-to-all | bytes 1048576 | tf_op jit(solution)/shard_map/all_to_all | solution.py:33
  123.2 3.0 %shard_map.76 = f32[8,32,128]{2,1,0:T(8,128)S(1)} custom-call(f32[32,32,128]{2,1,0:T(8,128)S(1)} %all_to_all.31.gathered, bf16[1,1024,512]{2,1,0:T(8,128)(2,1)S(1)} %get-tuple-element.59.refs_0_, bf16[1,1024,512]{2,1,0:T(8,128)(2,1)S(1)} %get-tuple-element.60.refs_1_, bf16[2,1024,512]{2,1,0:T(8,128)(2,1)S(1)} %get-tuple-element.61.refs_2_, ...), custom_call_target="tpu_custom_call" | custom-call | flops 1073741824 | bytes 16777216 | tf_op jit(solution)/shard_map/pallas_call | solution.py:264
  126.2 7.3 %collective-permute-start.13 = (f32[8,32,128]{2,1,0:T(8,128)S(1)}, f32[8,32,128]{2,1,0:T(8,128)S(1)}, u32[]{:S(2)}, u32[]{:S(2)}) collective-permute-start(f32[8,32,128]{2,1,0:T(8,128)S(1)} %shard_map.76), channel_id=1, source_target_pairs={{0,8},{8,0},{1,9},{9,1},{2,10},{10,2},{3,11},{11,3},{4,12},{12,4},... | collective-permute-start | bytes 393224 | tf_op jit(solution)/shard_map/ppermute | solution.py:29
  133.5 3.0 %shard_map.75 = f32[8,32,128]{2,1,0:T(8,128)S(1)} custom-call(f32[32,32,128]{2,1,0:T(8,128)S(1)} %all_to_all.31.gathered, bf16[1,1024,512]{2,1,0:T(8,128)(2,1)S(1)} %get-tuple-element.59.refs_0_, bf16[1,1024,512]{2,1,0:T(8,128)(2,1)S(1)} %get-tuple-element.60.refs_1_, bf16[2,1024,512]{2,1,0:T(8,128)(2,1)S(1)} %get-tuple-element.61.refs_2_, ...), custom_call_target="tpu_custom_call" | custom-call | flops 1073741824 | bytes 16777216 | tf_op jit(solution)/shard_map/pallas_call | solution.py:264
  136.5 0.0 collective-permute-done.13
  136.5 11.9 %all_to_all.32.arrived = f32[8,32,128]{2,1,0:T(8,128)S(1)} all-to-all(f32[8,32,128]{2,1,0:T(8,128)S(1)} %add.7), channel_id=1, replica_groups=mesh['x'=4,'y'=8,'c'=2,'z'=8] {'z'}, dimensions={0} | all-to-all | bytes 262144 | tf_op jit(solution)/shard_map/all_to_all | solution.py:33
  148.4 0.2 settle.1
  148.7 11.4 %all_to_all.33 = f32[16,1,128]{2,1,0:T(1,128)S(1)} all-to-all(f32[16,1,128]{2,1,0:T(1,128)S(1)} %broadcast_in_dim.19), channel_id=1, replica_groups=mesh['x'=4,'y'=8,'c'=2,'z'=8] {'y','c'}, dimensions={0} | all-to-all | bytes 16384 | tf_op jit(solution)/shard_map/all_to_all | solution.py:33
  160.1 11.6 %all_to_all.34.sums = f32[32,1,128]{2,1,0:T(1,128)S(1)} all-to-all(f32[32,1,128]{2,1,0:T(1,128)S(1)} %broadcast_in_dim.20), channel_id=1, replica_groups=mesh['x'=4,'y'=8,'c'=2,'z'=8] {'x','z'}, dimensions={0} | all-to-all | bytes 32768 | tf_op jit(solution)/shard_map/all_to_all | solution.py:33
  171.7 1.0 finish.1
  (14 shorter events, 0.2 us)
Async XLA Ops:
  3.8 29.9 %collective-permute-start.6 = (f32[128,128]{1,0:T(8,128)S(1)}, f32[128,128]{1,0:T(8,128)S(1)}, u32[]{:S(2)}, u32[]{:S(2)}) collective-permute-start(f32[128,128]{1,0:T(8,128)S(1)} %get-tuple-element.41.refs_0_), channel_id=1, source_target_pairs={{0,4},{1,5},{2,6},{3,7},{4,0},{5,1},{6,2},{7,3},{8,12},{9,13},{10,... | collective-permute-start | bytes 196616 | tf_op jit(solution)/shard_map/ppermute | solution.py:29
  15.2 12.1 %collective-permute-start.5 = (f32[128,128]{1,0:T(8,128)S(1)}, f32[128,128]{1,0:T(8,128)S(1)}, u32[]{:S(2)}, u32[]{:S(2)}) collective-permute-start(f32[128,128]{1,0:T(8,128)S(1)} %get-tuple-element.41.refs_0_), channel_id=1, source_target_pairs={{0,7},{1,0},{2,1},{3,2},{4,3},{5,4},{6,5},{7,6},{8,15},{9,8},{10,9... | collective-permute-start | bytes 196616 | tf_op jit(solution)/shard_map/ppermute | solution.py:29
  17.2 10.2 %collective-permute-start.4 = (f32[128,128]{1,0:T(8,128)S(1)}, f32[128,128]{1,0:T(8,128)S(1)}, u32[]{:S(2)}, u32[]{:S(2)}) collective-permute-start(f32[128,128]{1,0:T(8,128)S(1)} %get-tuple-element.41.refs_0_), channel_id=1, source_target_pairs={{0,1},{1,2},{2,3},{3,4},{4,5},{5,6},{6,7},{7,0},{8,9},{9,10},{10,1... | collective-permute-start | bytes 196616 | tf_op jit(solution)/shard_map/ppermute | solution.py:29
  20.5 26.1 %all-to-all-start = ((f32[8,160,128]{2,1,0:T(8,128)}), f32[8,160,128]{2,1,0:T(8,128)S(1)}, u32[]{:S(2)}, u32[]{:S(2)}) async-start(f32[8,160,128]{2,1,0:T(8,128)} %get-tuple-element.40), calls=%async_computation | async-start | bytes 1310720 | tf_op jit(solution)/shard_map/all_to_all | solution.py:33
  27.4 10.7 %collective-permute-start.8 = (f32[2,128,128]{2,1,0:T(8,128)S(1)}, f32[2,128,128]{2,1,0:T(8,128)S(1)}, u32[]{:S(2)}, u32[]{:S(2)}) collective-permute-start(f32[2,128,128]{2,1,0:T(8,128)S(1)} %get-tuple-element.78), channel_id=1, source_target_pairs={{0,6},{1,7},{2,0},{3,1},{4,2},{5,3},{6,4},{7,5},{8,14},{9,15},{10,... | collective-permute-start | bytes 393224 | tf_op jit(solution)/shard_map/ppermute | solution.py:29
  29.4 8.8 %collective-permute-start.7 = (f32[2,128,128]{2,1,0:T(8,128)S(1)}, f32[2,128,128]{2,1,0:T(8,128)S(1)}, u32[]{:S(2)}, u32[]{:S(2)}) collective-permute-start(f32[2,128,128]{2,1,0:T(8,128)S(1)} %get-tuple-element.79), channel_id=1, source_target_pairs={{0,2},{1,3},{2,4},{3,5},{4,6},{5,7},{6,0},{7,1},{8,10},{9,11},{10,... | collective-permute-start | bytes 393224 | tf_op jit(solution)/shard_map/ppermute | solution.py:29
  38.2 22.9 %collective-permute-start.9 = (f32[8,128,128]{2,1,0:T(8,128)S(1)}, f32[8,128,128]{2,1,0:T(8,128)S(1)}, u32[]{:S(2)}, u32[]{:S(2)}) collective-permute-start(f32[8,128,128]{2,1,0:T(8,128)S(1)} %constant_dynamic-update-slice_fusion), channel_id=1, source_target_pairs={{0,8},{8,0},{1,9},{9,1},{2,10},{10,2},{3,11},{11,3},{4,12},{12,4},... | collective-permute-start | bytes 1572872 | tf_op jit(solution)/shard_map/ppermute | solution.py:29
  46.7 17.9 %collective-permute-start.2 = (f32[4,160,128]{2,1,0:T(8,128)S(1)}, f32[4,160,128]{2,1,0:T(8,128)S(1)}, u32[]{:S(2)}, u32[]{:S(2)}) collective-permute-start(f32[4,160,128]{2,1,0:T(8,128)S(1)} %get-tuple-element.76), channel_id=1, source_target_pairs={{0,384},{128,0},{256,128},{384,256},{1,385},{129,1},{257,129},{385... | collective-permute-start | bytes 983048 | tf_op jit(solution)/shard_map/ppermute | solution.py:29
  51.1 16.9 %collective-permute-start = (f32[4,160,128]{2,1,0:T(8,128)S(1)}, f32[4,160,128]{2,1,0:T(8,128)S(1)}, u32[]{:S(2)}, u32[]{:S(2)}) collective-permute-start(f32[4,160,128]{2,1,0:T(8,128)S(1)} %get-tuple-element.77), channel_id=1, source_target_pairs={{0,128},{128,256},{256,384},{384,0},{1,129},{129,257},{257,385},{3... | collective-permute-start | bytes 983048 | tf_op jit(solution)/shard_map/ppermute | solution.py:29
  53.0 17.1 %collective-permute-start.11 = (f32[4,160,128]{2,1,0:T(8,128)S(1)}, f32[4,160,128]{2,1,0:T(8,128)S(1)}, u32[]{:S(2)}, u32[]{:S(2)}) collective-permute-start(f32[4,160,128]{2,1,0:T(8,128)S(1)} %get-tuple-element.76), channel_id=1, source_target_pairs={{0,128},{128,256},{256,384},{384,0},{1,129},{129,257},{257,385},{3... | collective-permute-start | bytes 983048 | tf_op jit(solution)/shard_map/ppermute | solution.py:29
  55.1 19.5 %collective-permute-start.10 = (f32[4,160,128]{2,1,0:T(8,128)S(1)}, f32[4,160,128]{2,1,0:T(8,128)S(1)}, u32[]{:S(2)}, u32[]{:S(2)}) collective-permute-start(f32[4,160,128]{2,1,0:T(8,128)S(1)} %get-tuple-element.77), channel_id=1, source_target_pairs={{0,384},{128,0},{256,128},{384,256},{1,385},{129,1},{257,129},{385... | collective-permute-start | bytes 983048 | tf_op jit(solution)/shard_map/ppermute | solution.py:29
  64.6 14.5 %collective-permute-start.3 = (f32[4,160,128]{2,1,0:T(8,128)S(1)}, f32[4,160,128]{2,1,0:T(8,128)S(1)}, u32[]{:S(2)}, u32[]{:S(2)}) collective-permute-start(f32[4,160,128]{2,1,0:T(8,128)S(1)} %collective-permute-done.2.refs_1_), channel_id=1, source_target_pairs={{0,384},{128,0},{256,128},{384,256},{1,385},{129,1},{257,129},{385... | collective-permute-start | bytes 983048 | tf_op jit(solution)/shard_map/ppermute | solution.py:29
  68.0 11.1 %collective-permute-start.1 = (f32[4,160,128]{2,1,0:T(8,128)S(1)}, f32[4,160,128]{2,1,0:T(8,128)S(1)}, u32[]{:S(2)}, u32[]{:S(2)}) collective-permute-start(f32[4,160,128]{2,1,0:T(8,128)S(1)} %collective-permute-done.refs_0_), channel_id=1, source_target_pairs={{0,128},{128,256},{256,384},{384,0},{1,129},{129,257},{257,385},{3... | collective-permute-start | bytes 983048 | tf_op jit(solution)/shard_map/ppermute | solution.py:29
  81.6 21.6 %copy-start = (f32[32,128]{1,0:T(8,128)S(1)}, f32[32,128]{1,0:T(8,128)}, u32[]{:S(2)}) copy-start(f32[32,128]{1,0:T(8,128)} %targets.5) | copy-start | bytes 49156
  81.6 7.8 %collective-permute-start.12 = (f32[8,32,128]{2,1,0:T(8,128)S(1)}, f32[8,32,128]{2,1,0:T(8,128)S(1)}, u32[]{:S(2)}, u32[]{:S(2)}) collective-permute-start(f32[8,32,128]{2,1,0:T(8,128)S(1)} %get-tuple-element.57), channel_id=1, source_target_pairs={{0,8},{8,0},{1,9},{9,1},{2,10},{10,2},{3,11},{11,3},{4,12},{12,4},... | collective-permute-start | bytes 393224 | tf_op jit(solution)/shard_map/ppermute | solution.py:29
  126.2 10.3 %collective-permute-start.13 = (f32[8,32,128]{2,1,0:T(8,128)S(1)}, f32[8,32,128]{2,1,0:T(8,128)S(1)}, u32[]{:S(2)}, u32[]{:S(2)}) collective-permute-start(f32[8,32,128]{2,1,0:T(8,128)S(1)} %shard_map.76), channel_id=1, source_target_pairs={{0,8},{8,0},{1,9},{9,1},{2,10},{10,2},{3,11},{11,3},{4,12},{12,4},... | collective-permute-start | bytes 393224 | tf_op jit(solution)/shard_map/ppermute | solution.py:29
where the time goes:
time: 173 us
  blocking collectives  68.5 us (40%)
  starting transfers between devices  65 us (38%)
  Pallas kernels  28.1 us (16%)
  waiting for transfers between devices  8.57 us (5%)
  between operations  2.25 us (1%)
    all_to_all x5, blocking collectives, exchange(): return lax.all_to_all(x, axes, 0, 0, tiled=True)  68.5 us
    ppermute x14, starting transfers between devices, shift(): lax.ppermute(value, axis, [(s, (s + steps) % count) for s in range(count)])  58.1 us
    pallas_call x4, Pallas kernels, more_chunk(): pl.pallas_call(functools.partial(more_kernel, tiles, last), in_specs=[VME...  13.9 us
    all_to_all x1, starting transfers between devices, exchange(): return lax.all_to_all(x, axes, 0, 0, tiled=True)  6.83 us
    pallas_call x2, Pallas kernels, second(): pl.pallas_call(functools.partial(second_kernel, tiles), in_specs=[VMEM] *...  6.01 us
    pallas_call x3, Pallas kernels, own_chunk(): pl.pallas_call(functools.partial(own_kernel, len(blocks)), in_specs=[VMEM...  4.69 us
    ppermute x14, waiting for transfers between devices, shift(): lax.ppermute(value, axis, [(s, (s + steps) % count) for s in range(count)])  4.51 us
    all_to_all x1, waiting for transfers between devices, exchange(): return lax.all_to_all(x, axes, 0, 0, tiled=True)  4.06 us
  transfers between devices with their start and end apart: 15, of which 2 were waited for; matrix products, arithmetic and copies ran while one was open for 0% of the time, Pallas kernels for 11%

commit v1 on v0

--- a/solution.py
+++ b/solution.py
@@ -148,8 +148,8 @@
             out[to * 4 + local] = piece
 
 
-def more_kernel(tiles, last, *refs):
-    cols, refs = refs[:2], refs[2:]
+def more_kernel(tiles, last, count, *refs):
+    cols, refs = refs[:count], refs[count:]
     lefts, befores, (out, high, low, right, right_sq, vecs) = refs[:6], refs[6:-6], refs[-6:]
     prepare_cols(cols, right, right_sq, vecs)
     for to, tile in enumerate(tiles):
@@ -204,8 +204,8 @@
 
 def more_chunk(tiles, cols, lefts, befores, last=False):
     return pl.pallas_call(
-        functools.partial(more_kernel, tiles, last),
-        in_specs=[VMEM] * (8 + len(befores)),
+        functools.partial(more_kernel, tiles, last, len(cols)),
+        in_specs=[VMEM] * (6 + len(cols) + len(befores)),
         out_specs=[VMEM] * 3,
         out_shape=made(tiles),
         scratch_shapes=RIGHT,
@@ -341,9 +341,8 @@
 def on_device(points, targets, lengthscales, outputscale, noise):
     near, own, aux = spread(points, lengthscales[None], targets, outputscale, noise)
     near = exchange(near, "y")
-    behind_low, ahead_high = shift(near[:4], "x", 1), shift(near[4:], "x", -1)
-    behind_high, ahead_low = shift(near[4:], "x", 1), shift(near[:4], "x", -1)
-    across = [shift(behind_low, "x", 1), shift(ahead_high, "x", -1)]
+    behind, ahead = shift(near, "x", 1), shift(near, "x", -1)
+    across = [shift(behind[:4], "x", 1), shift(ahead[4:], "x", -1)]
     below, above, far = shift(own, "z", 1), shift(own, "z", -1), shift(own, "z", 4)
     pairs = [shift(jnp.stack([below, own]), "z", 2), shift(jnp.stack([own, above]), "z", -2)]
     prepared = own_cols(near)
@@ -355,7 +354,7 @@
     chunks.append(own_chunk([other], prepared, THEIRS))
     pieces, highs, lows, left, left_sq = [list(part) for part in zip(*chunks)]
     lefts = [*left, *left_sq]
-    for cols in ([behind_low, behind_high], [ahead_low, ahead_high]):
+    for cols in ([behind], [ahead]):
         piece, high, low = more_chunk(ALL, cols, lefts, pieces)
         pieces = [piece]
         highs.append(high)
@@ -372,8 +371,8 @@
     mine = second(MINE, gathered, highs, lows)
     arrived = exchange(mine + theirs, "z")
     second_image, dots = settle(aux, arrived, targets, first)
-    sums = jnp.sum(to_each(dots[0:1], ("y", "c")), axis=0)
-    return tuple(finish(to_each(sums, ("x", "z")), targets, first, second_image))
+    sums = jnp.sum(to_each(dots[0:1], "z"), axis=0)
+    return tuple(finish(to_each(sums, ("x", "y", "c")), targets, first, second_image))
 
 
 def solution(mesh):

time: 173 us -> 178 us (1.029)
  waiting for transfers between devices: 8.57 us -> 13.6 us
  starting transfers between devices: 65 us -> 60.2 us
  blocking collectives: 68.5 us -> 72.6 us
    ppermute x14 -> x12, waiting for transfers between devices: 4.51 us -> 9.49 us  [shift(): lax.ppermute(value, axis, [(s, (s + steps) % count) for s in range(count)])]
    ppermute x14 -> x12, starting transfers between devices: 58.1 us -> 53.4 us  [shift(): lax.ppermute(value, axis, [(s, (s + steps) % count) for s in range(count)])]
    all_to_all x5, blocking collectives: 68.5 us -> 72.6 us  [exchange(): return lax.all_to_all(x, axes, 0, 0, tiled=True)]
  transfers between devices with their start and end apart: 15 -> 13, of which waited for: 2 -> 3; matrix products, arithmetic and copies ran while one was open for 0% -> 0% of each run, Pallas kernels for 11% -> 11%
where the time goes in v1:
time: 178 us; the launch traced here: 177 us
  blocking collectives  72.6 us (41%)
  starting transfers between devices  60.2 us (34%)
  Pallas kernels  28.4 us (16%)
  waiting for transfers between devices  13.6 us (8%)
  between operations  2.23 us (1%)
    all_to_all x5, blocking collectives, exchange(): return lax.all_to_all(x, axes, 0, 0, tiled=True)  72.6 us
    ppermute x12, starting transfers between devices, shift(): lax.ppermute(value, axis, [(s, (s + steps) % count) for s in range(count)])  53.4 us
    pallas_call x4, Pallas kernels, more_chunk(): pl.pallas_call(functools.partial(more_kernel, tiles, last, len(cols)), in...  14.1 us
    ppermute x12, waiting for transfers between devices, shift(): lax.ppermute(value, axis, [(s, (s + steps) % count) for s in range(count)])  9.49 us
    all_to_all x1, starting transfers between devices, exchange(): return lax.all_to_all(x, axes, 0, 0, tiled=True)  6.83 us
    pallas_call x2, Pallas kernels, second(): pl.pallas_call(functools.partial(second_kernel, tiles), in_specs=[VMEM] *...  6.01 us
    pallas_call x3, Pallas kernels, own_chunk(): pl.pallas_call(functools.partial(own_kernel, len(blocks)), in_specs=[VMEM...  4.73 us
    all_to_all x1, waiting for transfers between devices, exchange(): return lax.all_to_all(x, axes, 0, 0, tiled=True)  4.06 us
  transfers between devices with their start and end apart: 13, of which 3 were waited for; matrix products, arithmetic and copies ran while one was open for 0% of the time, Pallas kernels for 11%

profile of v1, /device:TPU:1, one launch (start us, length us, event | category | flops | bytes accessed | tf_op | source)
XLA Modules:
  0.0 177.2 jit_solution(2053787526809462853)
XLA Ops:
  1.9 1.9 %spread.1 = (f32[8,160,128]{2,1,0:T(8,128)}, f32[128,128]{1,0:T(8,128)S(1)}, f32[8,128]{1,0:T(8,128)S(1)}) custom-call(f32[128,128]{1,0:T(8,128)} %points_in.1, f32[1,128]{1,0:T(1,128)} %bitcast.16, f32[32,128]{1,0:T(8,128)} %targets.5, f32[1]{0:T(128)S(6)} %copy.13.scale, f32[1]{0:T(128)S(6)} %copy.14.noise), custom_call_target="tpu_custom_call" | custom-call | tf_op jit(solution)/shard_map/spread/pallas_call | solution.py:68
  3.8 11.5 %collective-permute-start.6 = (f32[128,128]{1,0:T(8,128)S(1)}, f32[128,128]{1,0:T(8,128)S(1)}, u32[]{:S(2)}, u32[]{:S(2)}) collective-permute-start(f32[128,128]{1,0:T(8,128)S(1)} %get-tuple-element.41.refs_0_), channel_id=1, source_target_pairs={{0,4},{1,5},{2,6},{3,7},{4,0},{5,1},{6,2},{7,3},{8,12},{9,13},{10,... | collective-permute-start | bytes 196616 | tf_op jit(solution)/shard_map/ppermute | solution.py:29
  15.2 2.0 %collective-permute-start.5 = (f32[128,128]{1,0:T(8,128)S(1)}, f32[128,128]{1,0:T(8,128)S(1)}, u32[]{:S(2)}, u32[]{:S(2)}) collective-permute-start(f32[128,128]{1,0:T(8,128)S(1)} %get-tuple-element.41.refs_0_), channel_id=1, source_target_pairs={{0,7},{1,0},{2,1},{3,2},{4,3},{5,4},{6,5},{7,6},{8,15},{9,8},{10,9... | collective-permute-start | bytes 196616 | tf_op jit(solution)/shard_map/ppermute | solution.py:29
  17.2 3.3 %collective-permute-start.4 = (f32[128,128]{1,0:T(8,128)S(1)}, f32[128,128]{1,0:T(8,128)S(1)}, u32[]{:S(2)}, u32[]{:S(2)}) collective-permute-start(f32[128,128]{1,0:T(8,128)S(1)} %get-tuple-element.41.refs_0_), channel_id=1, source_target_pairs={{0,1},{1,2},{2,3},{3,4},{4,5},{5,6},{6,7},{7,0},{8,9},{9,10},{10,1... | collective-permute-start | bytes 196616 | tf_op jit(solution)/shard_map/ppermute | solution.py:29
  20.5 6.8 %all-to-all-start = ((f32[8,160,128]{2,1,0:T(8,128)}), f32[8,160,128]{2,1,0:T(8,128)S(1)}, u32[]{:S(2)}, u32[]{:S(2)}) async-start(f32[8,160,128]{2,1,0:T(8,128)} %get-tuple-element.40), calls=%async_computation | async-start | bytes 1310720 | tf_op jit(solution)/shard_map/all_to_all | solution.py:33
  27.4 0.0 collective-permute-done.5.refs_2_
  27.4 0.0 collective-permute-done.4.refs_1_
  27.4 1.9 %collective-permute-start.8 = (f32[2,128,128]{2,1,0:T(8,128)S(1)}, f32[2,128,128]{2,1,0:T(8,128)S(1)}, u32[]{:S(2)}, u32[]{:S(2)}) collective-permute-start(f32[2,128,128]{2,1,0:T(8,128)S(1)} %get-tuple-element.76), channel_id=1, source_target_pairs={{0,6},{1,7},{2,0},{3,1},{4,2},{5,3},{6,4},{7,5},{8,14},{9,15},{10,... | collective-permute-start | bytes 393224 | tf_op jit(solution)/shard_map/ppermute | solution.py:29
  29.4 4.2 %collective-permute-start.7 = (f32[2,128,128]{2,1,0:T(8,128)S(1)}, f32[2,128,128]{2,1,0:T(8,128)S(1)}, u32[]{:S(2)}, u32[]{:S(2)}) collective-permute-start(f32[2,128,128]{2,1,0:T(8,128)S(1)} %get-tuple-element.77), channel_id=1, source_target_pairs={{0,2},{1,3},{2,4},{3,5},{4,6},{5,7},{6,0},{7,1},{8,10},{9,11},{10,... | collective-permute-start | bytes 393224 | tf_op jit(solution)/shard_map/ppermute | solution.py:29
  33.7 0.0 collective-permute-done.6.refs_3_
  33.7 4.5 %collective-permute-done.7.refs_0_ = f32[2,128,128]{2,1,0:T(8,128)S(1)} collective-permute-done((f32[2,128,128]{2,1,0:T(8,128)S(1)}, f32[2,128,128]{2,1,0:T(8,128)S(1)}, u32[]{:S(2)}, u32[]{:S(2)}) %collective-permute-start.7) | collective-permute-done | bytes 131104 | tf_op jit(solution)/shard_map/ppermute | solution.py:29
  38.2 0.0 collective-permute-done.8.refs_1_
  38.2 4.4 %collective-permute-start.9 = (f32[8,128,128]{2,1,0:T(8,128)S(1)}, f32[8,128,128]{2,1,0:T(8,128)S(1)}, u32[]{:S(2)}, u32[]{:S(2)}) collective-permute-start(f32[8,128,128]{2,1,0:T(8,128)S(1)} %constant_dynamic-update-slice_fusion), channel_id=1, source_target_pairs={{0,8},{8,0},{1,9},{9,1},{2,10},{10,2},{3,11},{11,3},{4,12},{12,4},... | collective-permute-start | bytes 1572872 | tf_op jit(solution)/shard_map/ppermute | solution.py:29
  42.6 4.1 %all-to-all-done.cols = f32[8,160,128]{2,1,0:T(8,128)S(1)} async-done(((f32[8,160,128]{2,1,0:T(8,128)}), f32[8,160,128]{2,1,0:T(8,128)S(1)}, u32[]{:S(2)}, u32[]{:S(2)}) %all-to-all-start) | async-done | bytes 655392 | tf_op jit(solution)/shard_map/all_to_all | solution.py:33
  46.6 4.4 %collective-permute-start.2 = (f32[8,160,128]{2,1,0:T(8,128)S(1)}, f32[8,160,128]{2,1,0:T(8,128)S(1)}, u32[]{:S(2)}, u32[]{:S(2)}) collective-permute-start(f32[8,160,128]{2,1,0:T(8,128)S(1)} %all-to-all-done.cols), channel_id=1, source_target_pairs={{0,384},{128,0},{256,128},{384,256},{1,385},{129,1},{257,129},{385... | collective-permute-start | bytes 1966088 | tf_op jit(solution)/shard_map/ppermute | solution.py:29
  51.0 1.9 %collective-permute-start = (f32[8,160,128]{2,1,0:T(8,128)S(1)}, f32[8,160,128]{2,1,0:T(8,128)S(1)}, u32[]{:S(2)}, u32[]{:S(2)}) collective-permute-start(f32[8,160,128]{2,1,0:T(8,128)S(1)} %all-to-all-done.cols), channel_id=1, source_target_pairs={{0,128},{128,256},{256,384},{384,0},{1,129},{129,257},{257,385},{3... | collective-permute-start | bytes 1966088 | tf_op jit(solution)/shard_map/ppermute | solution.py:29
  52.9 0.4 own_cols.1
  53.4 1.2 shard_map.69
  54.5 1.2 shard_map.68
  55.8 0.0 collective-permute-done.9.refs_0_
  55.8 2.3 %shard_map.70 = (f32[8,32,128]{2,1,0:T(8,128)S(1)}, bf16[2,1024,512]{2,1,0:T(8,128)(2,1)S(1)}, bf16[2,1024,512]{2,1,0:T(8,128)(2,1)S(1)}, bf16[2,512,512]{2,1,0:T(8,128)(2,1)S(1)}, f32[2,1,512]{2,1,0:T(1,128)S(1)}) custom-call(f32[8,128,128]{2,1,0:T(8,128)S(1)} %collective-permute-done.9.refs_0_, ...), custom_call_target="tpu_custom_call" | custom-call | flops 1610612736 | bytes 4194304 | tf_op jit(solution)/shard_map/pallas_call | solution.py:195
  58.1 5.0 %collective-permute-done.2.refs_0_ = f32[8,160,128]{2,1,0:T(8,128)S(1)} collective-permute-done((f32[8,160,128]{2,1,0:T(8,128)S(1)}, f32[8,160,128]{2,1,0:T(8,128)S(1)}, u32[]{:S(2)}, u32[]{:S(2)}) %collective-permute-start.2) | collective-permute-done | bytes 655392 | tf_op jit(solution)/shard_map/ppermute | solution.py:29
  63.1 5.3 %collective-permute-start.3 = (f32[4,160,128]{2,1,0:T(8,128)S(1)}, f32[4,160,128]{2,1,0:T(8,128)S(1)}, u32[]{:S(2)}, u32[]{:S(2)}) collective-permute-start(f32[4,160,128]{2,1,0:T(8,128)S(1)} %slice.13), channel_id=1, source_target_pairs={{0,384},{128,0},{256,128},{384,256},{1,385},{129,1},{257,129},{385... | collective-permute-start | bytes 983048 | tf_op jit(solution)/shard_map/ppermute | solution.py:29
  68.4 0.0 collective-permute-done.refs_0_
  68.5 2.1 %collective-permute-start.1 = (f32[4,160,128]{2,1,0:T(8,128)S(1)}, f32[4,160,128]{2,1,0:T(8,128)S(1)}, u32[]{:S(2)}, u32[]{:S(2)}) collective-permute-start(f32[4,160,128]{2,1,0:T(8,128)S(1)} %slice.12), channel_id=1, source_target_pairs={{0,128},{128,256},{256,384},{384,0},{1,129},{129,257},{257,385},{3... | collective-permute-start | bytes 983048 | tf_op jit(solution)/shard_map/ppermute | solution.py:29
  70.6 4.5 %shard_map.71 = (f32[16,32,128]{2,1,0:T(8,128)S(1)}, bf16[4,1024,512]{2,1,0:T(8,128)(2,1)S(1)}, bf16[4,1024,512]{2,1,0:T(8,128)(2,1)S(1)}) custom-call(f32[8,160,128]{2,1,0:T(8,128)S(1)} %collective-permute-done.refs_0_, bf16[1,512,512]{2,1,0:T(8,128)(2,1)S(1)} %get-tuple-element.45.refs_1_.refs_2_, ...), custom_call_target="tpu_custom_call" | custom-call | flops 3221225472 | bytes 8388608 | tf_op jit(solution)/shard_map/pallas_call | solution.py:206
  75.1 4.6 %shard_map.72 = (f32[16,32,128]{2,1,0:T(8,128)S(1)}, bf16[4,1024,512]{2,1,0:T(8,128)(2,1)S(1)}, bf16[4,1024,512]{2,1,0:T(8,128)(2,1)S(1)}) custom-call(f32[8,160,128]{2,1,0:T(8,128)S(1)} %collective-permute-done.2.refs_0_, bf16[1,512,512]{2,1,0:T(8,128)(2,1)S(1)} %get-tuple-element.45.refs_1_.refs_2_, ...), custom_call_target="tpu_custom_call" | custom-call | flops 3221225472 | bytes 8388608 | tf_op jit(solution)/shard_map/pallas_call | solution.py:206
  79.7 0.0 collective-permute-done.3.refs_1_
  79.7 0.0 collective-permute-done.1.refs_0_
  79.8 2.5 %shard_map.74 = (f32[8,32,128]{2,1,0:T(8,128)S(1)}, bf16[2,1024,512]{2,1,0:T(8,128)(2,1)S(1)}, bf16[2,1024,512]{2,1,0:T(8,128)(2,1)S(1)}) custom-call(f32[4,160,128]{2,1,0:T(8,128)S(1)} %collective-permute-done.1.refs_0_, f32[4,160,128]{2,1,0:T(8,128)S(1)} %collective-permute-done.3.refs_1_, bf16[1,512,512]{2,1,0:T(8,128)(2,1)S(1)} %get-tuple-element.45.refs_1_.refs_2_, ...), custom_call_target="tpu_custom_call" | custom-call | flops 1610612736 | bytes 4194304 | tf_op jit(solution)/shard_map/pallas_call | solution.py:206
  82.2 0.0 copy-start
  82.2 5.0 %collective-permute-start.10 = (f32[8,32,128]{2,1,0:T(8,128)S(1)}, f32[8,32,128]{2,1,0:T(8,128)S(1)}, u32[]{:S(2)}, u32[]{:S(2)}) collective-permute-start(f32[8,32,128]{2,1,0:T(8,128)S(1)} %get-tuple-element.57), channel_id=1, source_target_pairs={{0,8},{8,0},{1,9},{9,1},{2,10},{10,2},{3,11},{11,3},{4,12},{12,4},... | collective-permute-start | bytes 393224 | tf_op jit(solution)/shard_map/ppermute | solution.py:29
  87.3 2.5 %shard_map.73 = (f32[8,32,128]{2,1,0:T(8,128)S(1)}, bf16[2,1024,512]{2,1,0:T(8,128)(2,1)S(1)}, bf16[2,1024,512]{2,1,0:T(8,128)(2,1)S(1)}) custom-call(f32[4,160,128]{2,1,0:T(8,128)S(1)} %collective-permute-done.1.refs_0_, f32[4,160,128]{2,1,0:T(8,128)S(1)} %collective-permute-done.3.refs_1_, bf16[1,512,512]{2,1,0:T(8,128)(2,1)S(1)} %get-tuple-element.45.refs_1_.refs_2_, ...), custom_call_target="tpu_custom_call" | custom-call | flops 1610612736 | bytes 4194304 | tf_op jit(solution)/shard_map/pallas_call | solution.py:206
  89.8 0.0 collective-permute-done.10
  89.8 14.1 %all_to_all.30.arrived = f32[8,32,128]{2,1,0:T(8,128)S(1)} all-to-all(f32[8,32,128]{2,1,0:T(8,128)S(1)} %add.6), channel_id=1, replica_groups=mesh['x'=4,'y'=8,'c'=2,'z'=8] {'z'}, dimensions={0} | all-to-all | bytes 262144 | tf_op jit(solution)/shard_map/all_to_all | solution.py:33
  103.9 0.0 copy-done
  103.9 0.1 between.1
  104.0 21.6 %all_to_all.31.gathered = f32[32,32,128]{2,1,0:T(8,128)S(1)} all-to-all(f32[32,32,128]{2,1,0:T(8,128)S(1)} %get-tuple-element.58), channel_id=1, replica_groups=mesh['x'=4,'y'=8,'c'=2,'z'=8] {'x','y'}, dimensions={0} | all-to-all | bytes 1048576 | tf_op jit(solution)/shard_map/all_to_all | solution.py:33
  125.6 3.0 %shard_map.76 = f32[8,32,128]{2,1,0:T(8,128)S(1)} custom-call(f32[32,32,128]{2,1,0:T(8,128)S(1)} %all_to_all.31.gathered, bf16[1,1024,512]{2,1,0:T(8,128)(2,1)S(1)} %get-tuple-element.59.refs_0_, bf16[1,1024,512]{2,1,0:T(8,128)(2,1)S(1)} %get-tuple-element.60.refs_1_, bf16[2,1024,512]{2,1,0:T(8,128)(2,1)S(1)} %get-tuple-element.61.refs_2_, ...), custom_call_target="tpu_custom_call" | custom-call | flops 1073741824 | bytes 16777216 | tf_op jit(solution)/shard_map/pallas_call | solution.py:264
  128.6 7.3 %collective-permute-start.11 = (f32[8,32,128]{2,1,0:T(8,128)S(1)}, f32[8,32,128]{2,1,0:T(8,128)S(1)}, u32[]{:S(2)}, u32[]{:S(2)}) collective-permute-start(f32[8,32,128]{2,1,0:T(8,128)S(1)} %shard_map.76), channel_id=1, source_target_pairs={{0,8},{8,0},{1,9},{9,1},{2,10},{10,2},{3,11},{11,3},{4,12},{12,4},... | collective-permute-start | bytes 393224 | tf_op jit(solution)/shard_map/ppermute | solution.py:29
  135.9 3.0 %shard_map.75 = f32[8,32,128]{2,1,0:T(8,128)S(1)} custom-call(f32[32,32,128]{2,1,0:T(8,128)S(1)} %all_to_all.31.gathered, bf16[1,1024,512]{2,1,0:T(8,128)(2,1)S(1)} %get-tuple-element.59.refs_0_, bf16[1,1024,512]{2,1,0:T(8,128)(2,1)S(1)} %get-tuple-element.60.refs_1_, bf16[2,1024,512]{2,1,0:T(8,128)(2,1)S(1)} %get-tuple-element.61.refs_2_, ...), custom_call_target="tpu_custom_call" | custom-call | flops 1073741824 | bytes 16777216 | tf_op jit(solution)/shard_map/pallas_call | solution.py:264
  138.9 0.0 collective-permute-done.11
  139.0 11.9 %all_to_all.32.arrived = f32[8,32,128]{2,1,0:T(8,128)S(1)} all-to-all(f32[8,32,128]{2,1,0:T(8,128)S(1)} %add.7), channel_id=1, replica_groups=mesh['x'=4,'y'=8,'c'=2,'z'=8] {'z'}, dimensions={0} | all-to-all | bytes 262144 | tf_op jit(solution)/shard_map/all_to_all | solution.py:33
  150.8 0.2 settle.1
  151.1 8.9 %all_to_all.33 = f32[8,1,128]{2,1,0:T(1,128)S(1)} all-to-all(f32[8,1,128]{2,1,0:T(1,128)S(1)} %broadcast_in_dim.19), channel_id=1, replica_groups=mesh['x'=4,'y'=8,'c'=2,'z'=8] {'z'}, dimensions={0} | all-to-all | bytes 8192 | tf_op jit(solution)/shard_map/all_to_all | solution.py:33
  160.1 16.1 %all_to_all.34.sums = f32[64,1,128]{2,1,0:T(1,128)S(1)} all-to-all(f32[64,1,128]{2,1,0:T(1,128)S(1)} %broadcast_in_dim.20), channel_id=1, replica_groups=mesh['x'=4,'y'=8,'c'=2,'z'=8] {'x','y','c'}, dimensions={0} | all-to-all | bytes 65536 | tf_op jit(solution)/shard_map/all_to_all | solution.py:33
  176.2 1.0 finish.1
  (15 shorter events, 0.2 us)
Async XLA Ops:
  3.8 29.9 %collective-permute-start.6 = (f32[128,128]{1,0:T(8,128)S(1)}, f32[128,128]{1,0:T(8,128)S(1)}, u32[]{:S(2)}, u32[]{:S(2)}) collective-permute-start(f32[128,128]{1,0:T(8,128)S(1)} %get-tuple-element.41.refs_0_), channel_id=1, source_target_pairs={{0,4},{1,5},{2,6},{3,7},{4,0},{5,1},{6,2},{7,3},{8,12},{9,13},{10,... | collective-permute-start | bytes 196616 | tf_op jit(solution)/shard_map/ppermute | solution.py:29
  15.2 12.1 %collective-permute-start.5 = (f32[128,128]{1,0:T(8,128)S(1)}, f32[128,128]{1,0:T(8,128)S(1)}, u32[]{:S(2)}, u32[]{:S(2)}) collective-permute-start(f32[128,128]{1,0:T(8,128)S(1)} %get-tuple-element.41.refs_0_), channel_id=1, source_target_pairs={{0,7},{1,0},{2,1},{3,2},{4,3},{5,4},{6,5},{7,6},{8,15},{9,8},{10,9... | collective-permute-start | bytes 196616 | tf_op jit(solution)/shard_map/ppermute | solution.py:29
  17.2 10.2 %collective-permute-start.4 = (f32[128,128]{1,0:T(8,128)S(1)}, f32[128,128]{1,0:T(8,128)S(1)}, u32[]{:S(2)}, u32[]{:S(2)}) collective-permute-start(f32[128,128]{1,0:T(8,128)S(1)} %get-tuple-element.41.refs_0_), channel_id=1, source_target_pairs={{0,1},{1,2},{2,3},{3,4},{4,5},{5,6},{6,7},{7,0},{8,9},{9,10},{10,1... | collective-permute-start | bytes 196616 | tf_op jit(solution)/shard_map/ppermute | solution.py:29
  20.5 26.1 %all-to-all-start = ((f32[8,160,128]{2,1,0:T(8,128)}), f32[8,160,128]{2,1,0:T(8,128)S(1)}, u32[]{:S(2)}, u32[]{:S(2)}) async-start(f32[8,160,128]{2,1,0:T(8,128)} %get-tuple-element.40), calls=%async_computation | async-start | bytes 1310720 | tf_op jit(solution)/shard_map/all_to_all | solution.py:33
  27.4 10.7 %collective-permute-start.8 = (f32[2,128,128]{2,1,0:T(8,128)S(1)}, f32[2,128,128]{2,1,0:T(8,128)S(1)}, u32[]{:S(2)}, u32[]{:S(2)}) collective-permute-start(f32[2,128,128]{2,1,0:T(8,128)S(1)} %get-tuple-element.76), channel_id=1, source_target_pairs={{0,6},{1,7},{2,0},{3,1},{4,2},{5,3},{6,4},{7,5},{8,14},{9,15},{10,... | collective-permute-start | bytes 393224 | tf_op jit(solution)/shard_map/ppermute | solution.py:29
  29.4 8.8 %collective-permute-start.7 = (f32[2,128,128]{2,1,0:T(8,128)S(1)}, f32[2,128,128]{2,1,0:T(8,128)S(1)}, u32[]{:S(2)}, u32[]{:S(2)}) collective-permute-start(f32[2,128,128]{2,1,0:T(8,128)S(1)} %get-tuple-element.77), channel_id=1, source_target_pairs={{0,2},{1,3},{2,4},{3,5},{4,6},{5,7},{6,0},{7,1},{8,10},{9,11},{10,... | collective-permute-start | bytes 393224 | tf_op jit(solution)/shard_map/ppermute | solution.py:29
  38.2 17.6 %collective-permute-start.9 = (f32[8,128,128]{2,1,0:T(8,128)S(1)}, f32[8,128,128]{2,1,0:T(8,128)S(1)}, u32[]{:S(2)}, u32[]{:S(2)}) collective-permute-start(f32[8,128,128]{2,1,0:T(8,128)S(1)} %constant_dynamic-update-slice_fusion), channel_id=1, source_target_pairs={{0,8},{8,0},{1,9},{9,1},{2,10},{10,2},{3,11},{11,3},{4,12},{12,4},... | collective-permute-start | bytes 1572872 | tf_op jit(solution)/shard_map/ppermute | solution.py:29
  46.6 16.4 %collective-permute-start.2 = (f32[8,160,128]{2,1,0:T(8,128)S(1)}, f32[8,160,128]{2,1,0:T(8,128)S(1)}, u32[]{:S(2)}, u32[]{:S(2)}) collective-permute-start(f32[8,160,128]{2,1,0:T(8,128)S(1)} %all-to-all-done.cols), channel_id=1, source_target_pairs={{0,384},{128,0},{256,128},{384,256},{1,385},{129,1},{257,129},{385... | collective-permute-start | bytes 1966088 | tf_op jit(solution)/shard_map/ppermute | solution.py:29
  51.0 17.4 %collective-permute-start = (f32[8,160,128]{2,1,0:T(8,128)S(1)}, f32[8,160,128]{2,1,0:T(8,128)S(1)}, u32[]{:S(2)}, u32[]{:S(2)}) collective-permute-start(f32[8,160,128]{2,1,0:T(8,128)S(1)} %all-to-all-done.cols), channel_id=1, source_target_pairs={{0,128},{128,256},{256,384},{384,0},{1,129},{129,257},{257,385},{3... | collective-permute-start | bytes 1966088 | tf_op jit(solution)/shard_map/ppermute | solution.py:29
  63.1 16.6 %collective-permute-start.3 = (f32[4,160,128]{2,1,0:T(8,128)S(1)}, f32[4,160,128]{2,1,0:T(8,128)S(1)}, u32[]{:S(2)}, u32[]{:S(2)}) collective-permute-start(f32[4,160,128]{2,1,0:T(8,128)S(1)} %slice.13), channel_id=1, source_target_pairs={{0,384},{128,0},{256,128},{384,256},{1,385},{129,1},{257,129},{385... | collective-permute-start | bytes 983048 | tf_op jit(solution)/shard_map/ppermute | solution.py:29
  68.5 11.3 %collective-permute-start.1 = (f32[4,160,128]{2,1,0:T(8,128)S(1)}, f32[4,160,128]{2,1,0:T(8,128)S(1)}, u32[]{:S(2)}, u32[]{:S(2)}) collective-permute-start(f32[4,160,128]{2,1,0:T(8,128)S(1)} %slice.12), channel_id=1, source_target_pairs={{0,128},{128,256},{256,384},{384,0},{1,129},{129,257},{257,385},{3... | collective-permute-start | bytes 983048 | tf_op jit(solution)/shard_map/ppermute | solution.py:29
  82.2 21.7 %copy-start = (f32[32,128]{1,0:T(8,128)S(1)}, f32[32,128]{1,0:T(8,128)}, u32[]{:S(2)}) copy-start(f32[32,128]{1,0:T(8,128)} %targets.5) | copy-start | bytes 49156
  82.2 7.6 %collective-permute-start.10 = (f32[8,32,128]{2,1,0:T(8,128)S(1)}, f32[8,32,128]{2,1,0:T(8,128)S(1)}, u32[]{:S(2)}, u32[]{:S(2)}) collective-permute-start(f32[8,32,128]{2,1,0:T(8,128)S(1)} %get-tuple-element.57), channel_id=1, source_target_pairs={{0,8},{8,0},{1,9},{9,1},{2,10},{10,2},{3,11},{11,3},{4,12},{12,4},... | collective-permute-start | bytes 393224 | tf_op jit(solution)/shard_map/ppermute | solution.py:29
  128.6 10.3 %collective-permute-start.11 = (f32[8,32,128]{2,1,0:T(8,128)S(1)}, f32[8,32,128]{2,1,0:T(8,128)S(1)}, u32[]{:S(2)}, u32[]{:S(2)}) collective-permute-start(f32[8,32,128]{2,1,0:T(8,128)S(1)} %shard_map.76), channel_id=1, source_target_pairs={{0,8},{8,0},{1,9},{9,1},{2,10},{10,2},{3,11},{11,3},{4,12},{12,4},... | collective-permute-start | bytes 393224 | tf_op jit(solution)/shard_map/ppermute | solution.py:29

commit v2 on v1

--- a/solution.py
+++ b/solution.py
@@ -333,6 +333,30 @@
     )(sums, targets, first, second_image)
 
 
+def received_kernel(behind, ahead, out):
+    odd = lax.rem(lax.axis_index("z"), 2) == 1
+
+    @pl.when(odd)
+    def _():
+        out[...] = ahead[4:]
+
+    @pl.when(jnp.logical_not(odd))
+    def _():
+        out[...] = behind[4:]
+
+
+def received(behind, ahead):
+    return pl.pallas_call(
+        received_kernel,
+        in_specs=[VMEM] * 2,
+        out_specs=VMEM,
+        out_shape=jax.ShapeDtypeStruct((4, *behind.shape[1:]), F32),
+        compiler_params=PARAMS,
+        cost_estimate=cost(0, 1 << 20, 0),
+        name="received",
+    )(behind, ahead)
+
+
 def to_each(x, axes):
     peers = lax.axis_size(axes)
     return exchange(jnp.broadcast_to(x[None], (peers, *x.shape)), axes)
@@ -342,7 +366,10 @@
     near, own, aux = spread(points, lengthscales[None], targets, outputscale, noise)
     near = exchange(near, "y")
     behind, ahead = shift(near, "x", 1), shift(near, "x", -1)
-    across = [shift(behind[:4], "x", 1), shift(ahead[4:], "x", -1)]
+    across = [shift(near[:4], "x", 2)]
+    onward = received(behind, ahead)
+    hops = [(x * 8 + z, (x + (3 if z % 2 else 1)) % 4 * 8 + z) for x in range(4) for z in range(8)]
+    across.append(lax.ppermute(onward, ("x", "z"), hops))
     below, above, far = shift(own, "z", 1), shift(own, "z", -1), shift(own, "z", 4)
     pairs = [shift(jnp.stack([below, own]), "z", 2), shift(jnp.stack([own, above]), "z", -2)]
     prepared = own_cols(near)
@@ -371,8 +398,8 @@
     mine = second(MINE, gathered, highs, lows)
     arrived = exchange(mine + theirs, "z")
     second_image, dots = settle(aux, arrived, targets, first)
-    sums = jnp.sum(to_each(dots[0:1], "z"), axis=0)
-    return tuple(finish(to_each(sums, ("x", "y", "c")), targets, first, second_image))
+    sums = jnp.sum(to_each(dots[0:1], ("y", "c")), axis=0)
+    return tuple(finish(to_each(sums, ("x", "z")), targets, first, second_image))
 
 
 def solution(mesh):

time: 178 us -> 182 us (1.022)
  starting transfers between devices: 60.2 us -> 63.2 us
  waiting for transfers between devices: 13.6 us -> 16.5 us
  blocking collectives: 72.6 us -> 70.3 us
    ppermute x12 -> x11, waiting for transfers between devices: 9.49 us -> 11.8 us  [shift(): lax.ppermute(value, axis, [(s, (s + steps) % count) for s in range(count)])]
    all_to_all x5, blocking collectives: 72.6 us -> 70.3 us  [exchange(): return lax.all_to_all(x, axes, 0, 0, tiled=True)]
    ppermute x0 -> x1, starting transfers between devices: none -> 2.1 us  [on_device(): across.append(lax.ppermute(onward, ('x', 'z'), hops))]
    ppermute x12 -> x11, starting transfers between devices: 53.4 us -> 54.3 us  [shift(): lax.ppermute(value, axis, [(s, (s + steps) % count) for s in range(count)])]
  transfers between devices with their start and end apart: 13 -> 13, of which waited for: 3 -> 5; matrix products, arithmetic and copies ran while one was open for 0% -> 0% of each run, Pallas kernels for 11% -> 11%
where the time goes in v2:
time: 182 us; the launch traced here: 181 us
  blocking collectives  70.3 us (39%)
  starting transfers between devices  63.2 us (35%)
  Pallas kernels  28.5 us (16%)
  waiting for transfers between devices  16.5 us (9%)
  between operations  2.21 us (1%)
    all_to_all x5, blocking collectives, exchange(): return lax.all_to_all(x, axes, 0, 0, tiled=True)  70.3 us
    ppermute x11, starting transfers between devices, shift(): lax.ppermute(value, axis, [(s, (s + steps) % count) for s in range(count)])  54.3 us
    pallas_call x4, Pallas kernels, more_chunk(): pl.pallas_call(functools.partial(more_kernel, tiles, last, len(cols)), in...  14.2 us
    ppermute x11, waiting for transfers between devices, shift(): lax.ppermute(value, axis, [(s, (s + steps) % count) for s in range(count)])  11.8 us
    all_to_all x1, starting transfers between devices, exchange(): return lax.all_to_all(x, axes, 0, 0, tiled=True)  6.83 us
    pallas_call x2, Pallas kernels, second(): pl.pallas_call(functools.partial(second_kernel, tiles), in_specs=[VMEM] *...  6 us
    pallas_call x3, Pallas kernels, own_chunk(): pl.pallas_call(functools.partial(own_kernel, len(blocks)), in_specs=[VMEM...  4.74 us
    all_to_all x1, waiting for transfers between devices, exchange(): return lax.all_to_all(x, axes, 0, 0, tiled=True)  4.06 us
  transfers between devices with their start and end apart: 13, of which 5 were waited for; matrix products, arithmetic and copies ran while one was open for 0% of the time, Pallas kernels for 11%

profile of v2, /device:TPU:1, one launch (start us, length us, event | category | flops | bytes accessed | tf_op | source)
XLA Modules:
  0.0 180.9 jit_solution(15652431364446777484)
XLA Ops:
  1.9 1.9 %spread.1 = (f32[8,160,128]{2,1,0:T(8,128)}, f32[128,128]{1,0:T(8,128)S(1)}, f32[8,128]{1,0:T(8,128)S(1)}) custom-call(f32[128,128]{1,0:T(8,128)} %points_in.1, f32[1,128]{1,0:T(1,128)} %bitcast.16, f32[32,128]{1,0:T(8,128)} %targets.5, f32[1]{0:T(128)S(6)} %copy.13.scale, f32[1]{0:T(128)S(6)} %copy.14.noise), custom_call_target="tpu_custom_call" | custom-call | tf_op jit(solution)/shard_map/spread/pallas_call | solution.py:68
  3.8 11.5 %collective-permute-start.6 = (f32[128,128]{1,0:T(8,128)S(1)}, f32[128,128]{1,0:T(8,128)S(1)}, u32[]{:S(2)}, u32[]{:S(2)}) collective-permute-start(f32[128,128]{1,0:T(8,128)S(1)} %get-tuple-element.41.refs_0_), channel_id=1, source_target_pairs={{0,4},{1,5},{2,6},{3,7},{4,0},{5,1},{6,2},{7,3},{8,12},{9,13},{10,... | collective-permute-start | bytes 196616 | tf_op jit(solution)/shard_map/ppermute | solution.py:29
  15.2 2.0 %collective-permute-start.5 = (f32[128,128]{1,0:T(8,128)S(1)}, f32[128,128]{1,0:T(8,128)S(1)}, u32[]{:S(2)}, u32[]{:S(2)}) collective-permute-start(f32[128,128]{1,0:T(8,128)S(1)} %get-tuple-element.41.refs_0_), channel_id=1, source_target_pairs={{0,7},{1,0},{2,1},{3,2},{4,3},{5,4},{6,5},{7,6},{8,15},{9,8},{10,9... | collective-permute-start | bytes 196616 | tf_op jit(solution)/shard_map/ppermute | solution.py:29
  17.2 3.3 %collective-permute-start.4 = (f32[128,128]{1,0:T(8,128)S(1)}, f32[128,128]{1,0:T(8,128)S(1)}, u32[]{:S(2)}, u32[]{:S(2)}) collective-permute-start(f32[128,128]{1,0:T(8,128)S(1)} %get-tuple-element.41.refs_0_), channel_id=1, source_target_pairs={{0,1},{1,2},{2,3},{3,4},{4,5},{5,6},{6,7},{7,0},{8,9},{9,10},{10,1... | collective-permute-start | bytes 196616 | tf_op jit(solution)/shard_map/ppermute | solution.py:29
  20.5 6.8 %all-to-all-start = ((f32[8,160,128]{2,1,0:T(8,128)}), f32[8,160,128]{2,1,0:T(8,128)S(1)}, u32[]{:S(2)}, u32[]{:S(2)}) async-start(f32[8,160,128]{2,1,0:T(8,128)} %get-tuple-element.40), calls=%async_computation | async-start | bytes 1310720 | tf_op jit(solution)/shard_map/all_to_all | solution.py:33
  27.4 0.0 collective-permute-done.5.refs_2_
  27.4 0.0 collective-permute-done.4.refs_1_
  27.4 1.9 %collective-permute-start.8 = (f32[2,128,128]{2,1,0:T(8,128)S(1)}, f32[2,128,128]{2,1,0:T(8,128)S(1)}, u32[]{:S(2)}, u32[]{:S(2)}) collective-permute-start(f32[2,128,128]{2,1,0:T(8,128)S(1)} %get-tuple-element.76), channel_id=1, source_target_pairs={{0,6},{1,7},{2,0},{3,1},{4,2},{5,3},{6,4},{7,5},{8,14},{9,15},{10,... | collective-permute-start | bytes 393224 | tf_op jit(solution)/shard_map/ppermute | solution.py:29
  29.4 4.2 %collective-permute-start.7 = (f32[2,128,128]{2,1,0:T(8,128)S(1)}, f32[2,128,128]{2,1,0:T(8,128)S(1)}, u32[]{:S(2)}, u32[]{:S(2)}) collective-permute-start(f32[2,128,128]{2,1,0:T(8,128)S(1)} %get-tuple-element.77), channel_id=1, source_target_pairs={{0,2},{1,3},{2,4},{3,5},{4,6},{5,7},{6,0},{7,1},{8,10},{9,11},{10,... | collective-permute-start | bytes 393224 | tf_op jit(solution)/shard_map/ppermute | solution.py:29
  33.7 0.0 collective-permute-done.6.refs_3_
  33.7 4.5 %collective-permute-done.7.refs_0_ = f32[2,128,128]{2,1,0:T(8,128)S(1)} collective-permute-done((f32[2,128,128]{2,1,0:T(8,128)S(1)}, f32[2,128,128]{2,1,0:T(8,128)S(1)}, u32[]{:S(2)}, u32[]{:S(2)}) %collective-permute-start.7) | collective-permute-done | bytes 131104 | tf_op jit(solution)/shard_map/ppermute | solution.py:29
  38.2 0.0 collective-permute-done.8.refs_1_
  38.2 4.4 %collective-permute-start.9 = (f32[8,128,128]{2,1,0:T(8,128)S(1)}, f32[8,128,128]{2,1,0:T(8,128)S(1)}, u32[]{:S(2)}, u32[]{:S(2)}) collective-permute-start(f32[8,128,128]{2,1,0:T(8,128)S(1)} %constant_dynamic-update-slice_fusion), channel_id=1, source_target_pairs={{0,8},{8,0},{1,9},{9,1},{2,10},{10,2},{3,11},{11,3},{4,12},{12,4},... | collective-permute-start | bytes 1572872 | tf_op jit(solution)/shard_map/ppermute | solution.py:29
  42.6 4.1 %all-to-all-done.cols = f32[8,160,128]{2,1,0:T(8,128)S(1)} async-done(((f32[8,160,128]{2,1,0:T(8,128)}), f32[8,160,128]{2,1,0:T(8,128)S(1)}, u32[]{:S(2)}, u32[]{:S(2)}) %all-to-all-start) | async-done | bytes 655392 | tf_op jit(solution)/shard_map/all_to_all | solution.py:33
  46.6 4.4 %collective-permute-start.2 = (f32[8,160,128]{2,1,0:T(8,128)S(1)}, f32[8,160,128]{2,1,0:T(8,128)S(1)}, u32[]{:S(2)}, u32[]{:S(2)}) collective-permute-start(f32[8,160,128]{2,1,0:T(8,128)S(1)} %all-to-all-done.cols), channel_id=1, source_target_pairs={{0,384},{128,0},{256,128},{384,256},{1,385},{129,1},{257,129},{385... | collective-permute-start | bytes 1966088 | tf_op jit(solution)/shard_map/ppermute | solution.py:29
  51.0 1.9 %collective-permute-start.1 = (f32[8,160,128]{2,1,0:T(8,128)S(1)}, f32[8,160,128]{2,1,0:T(8,128)S(1)}, u32[]{:S(2)}, u32[]{:S(2)}) collective-permute-start(f32[8,160,128]{2,1,0:T(8,128)S(1)} %all-to-all-done.cols), channel_id=1, source_target_pairs={{0,128},{128,256},{256,384},{384,0},{1,129},{129,257},{257,385},{3... | collective-permute-start | bytes 1966088 | tf_op jit(solution)/shard_map/ppermute | solution.py:29
  53.0 3.6 %collective-permute-start = (f32[4,160,128]{2,1,0:T(8,128)S(1)}, f32[4,160,128]{2,1,0:T(8,128)S(1)}, u32[]{:S(2)}, u32[]{:S(2)}) collective-permute-start(f32[4,160,128]{2,1,0:T(8,128)S(1)} %slice.8), channel_id=1, source_target_pairs={{0,256},{128,384},{256,0},{384,128},{1,257},{129,385},{257,1},{385... | collective-permute-start | bytes 983048 | tf_op jit(solution)/shard_map/ppermute | solution.py:29
  56.6 0.4 own_cols.1
  57.0 1.2 shard_map.69
  58.2 1.2 shard_map.68
  59.4 0.0 collective-permute-done.9.refs_0_
  59.4 2.3 %shard_map.70 = (f32[8,32,128]{2,1,0:T(8,128)S(1)}, bf16[2,1024,512]{2,1,0:T(8,128)(2,1)S(1)}, bf16[2,1024,512]{2,1,0:T(8,128)(2,1)S(1)}, bf16[2,512,512]{2,1,0:T(8,128)(2,1)S(1)}, f32[2,1,512]{2,1,0:T(1,128)S(1)}) custom-call(f32[8,128,128]{2,1,0:T(8,128)S(1)} %collective-permute-done.9.refs_0_, ...), custom_call_target="tpu_custom_call" | custom-call | flops 1610612736 | bytes 4194304 | tf_op jit(solution)/shard_map/pallas_call | solution.py:195
  61.8 2.1 %collective-permute-done.2.ahead.refs_0_ = f32[8,160,128]{2,1,0:T(8,128)S(1)} collective-permute-done((f32[8,160,128]{2,1,0:T(8,128)S(1)}, f32[8,160,128]{2,1,0:T(8,128)S(1)}, u32[]{:S(2)}, u32[]{:S(2)}) %collective-permute-start.2) | collective-permute-done | bytes 655392 | tf_op jit(solution)/shard_map/ppermute | solution.py:29
  63.9 5.2 %collective-permute-done.1.behind.refs_0_ = f32[8,160,128]{2,1,0:T(8,128)S(1)} collective-permute-done((f32[8,160,128]{2,1,0:T(8,128)S(1)}, f32[8,160,128]{2,1,0:T(8,128)S(1)}, u32[]{:S(2)}, u32[]{:S(2)}) %collective-permute-start.1) | collective-permute-done | bytes 655392 | tf_op jit(solution)/shard_map/ppermute | solution.py:29
  69.1 2.1 %collective-permute-start.3 = (f32[4,160,128]{2,1,0:T(8,128)S(1)}, f32[4,160,128]{2,1,0:T(8,128)S(1)}, u32[]{:S(2)}, u32[]{:S(2)}) collective-permute-start(f32[4,160,128]{2,1,0:T(8,128)S(1)} %received.1), channel_id=1, source_target_pairs={{0,128},{1,385},{2,130},{3,387},{4,132},{5,389},{6,134},{7,391},{1... | collective-permute-start | bytes 983048 | tf_op jit(solution)/shard_map/ppermute | solution.py:372
  71.2 4.5 %shard_map.71 = (f32[16,32,128]{2,1,0:T(8,128)S(1)}, bf16[4,1024,512]{2,1,0:T(8,128)(2,1)S(1)}, bf16[4,1024,512]{2,1,0:T(8,128)(2,1)S(1)}) custom-call(f32[8,160,128]{2,1,0:T(8,128)S(1)} %collective-permute-done.1.behind.refs_0_, bf16[1,512,512]{2,1,0:T(8,128)(2,1)S(1)} %get-tuple-element.45.refs_1_.refs_2_, ...), custom_call_target="tpu_custom_call" | custom-call | flops 3221225472 | bytes 8388608 | tf_op jit(solution)/shard_map/pallas_call | solution.py:206
  75.8 4.7 %shard_map.72 = (f32[16,32,128]{2,1,0:T(8,128)S(1)}, bf16[4,1024,512]{2,1,0:T(8,128)(2,1)S(1)}, bf16[4,1024,512]{2,1,0:T(8,128)(2,1)S(1)}) custom-call(f32[8,160,128]{2,1,0:T(8,128)S(1)} %collective-permute-done.2.ahead.refs_0_, bf16[1,512,512]{2,1,0:T(8,128)(2,1)S(1)} %get-tuple-element.45.refs_1_.refs_2_, ...), custom_call_target="tpu_custom_call" | custom-call | flops 3221225472 | bytes 8388608 | tf_op jit(solution)/shard_map/pallas_call | solution.py:206
  80.4 0.0 collective-permute-done.refs_0_
  80.4 0.7 collective-permute-done.3.refs_1_
  81.1 2.5 %shard_map.74 = (f32[8,32,128]{2,1,0:T(8,128)S(1)}, bf16[2,1024,512]{2,1,0:T(8,128)(2,1)S(1)}, bf16[2,1024,512]{2,1,0:T(8,128)(2,1)S(1)}) custom-call(f32[4,160,128]{2,1,0:T(8,128)S(1)} %collective-permute-done.refs_0_, f32[4,160,128]{2,1,0:T(8,128)S(1)} %collective-permute-done.3.refs_1_, bf16[1,512,512]{2,1,0:T(8,128)(2,1)S(1)} %get-tuple-element.45.refs_1_.refs_2_, ...), custom_call_target="tpu_custom_call" | custom-call | flops 1610612736 | bytes 4194304 | tf_op jit(solution)/shard_map/pallas_call | solution.py:206
  83.6 0.0 copy-start
  83.7 9.8 %collective-permute-start.10 = (f32[8,32,128]{2,1,0:T(8,128)S(1)}, f32[8,32,128]{2,1,0:T(8,128)S(1)}, u32[]{:S(2)}, u32[]{:S(2)}) collective-permute-start(f32[8,32,128]{2,1,0:T(8,128)S(1)} %get-tuple-element.57), channel_id=1, source_target_pairs={{0,8},{8,0},{1,9},{9,1},{2,10},{10,2},{3,11},{11,3},{4,12},{12,4},... | collective-permute-start | bytes 393224 | tf_op jit(solution)/shard_map/ppermute | solution.py:29
  93.4 2.5 %shard_map.73 = (f32[8,32,128]{2,1,0:T(8,128)S(1)}, bf16[2,1024,512]{2,1,0:T(8,128)(2,1)S(1)}, bf16[2,1024,512]{2,1,0:T(8,128)(2,1)S(1)}) custom-call(f32[4,160,128]{2,1,0:T(8,128)S(1)} %collective-permute-done.refs_0_, f32[4,160,128]{2,1,0:T(8,128)S(1)} %collective-permute-done.3.refs_1_, bf16[1,512,512]{2,1,0:T(8,128)(2,1)S(1)} %get-tuple-element.45.refs_1_.refs_2_, ...), custom_call_target="tpu_custom_call" | custom-call | flops 1610612736 | bytes 4194304 | tf_op jit(solution)/shard_map/pallas_call | solution.py:206
  95.9 0.0 collective-permute-done.10
  95.9 14.5 %all_to_all.30.arrived = f32[8,32,128]{2,1,0:T(8,128)S(1)} all-to-all(f32[8,32,128]{2,1,0:T(8,128)S(1)} %add.6), channel_id=1, replica_groups=mesh['x'=4,'y'=8,'c'=2,'z'=8] {'z'}, dimensions={0} | all-to-all | bytes 262144 | tf_op jit(solution)/shard_map/all_to_all | solution.py:33
  110.4 0.0 copy-done
  110.4 0.1 between.1
  110.5 21.0 %all_to_all.31.gathered = f32[32,32,128]{2,1,0:T(8,128)S(1)} all-to-all(f32[32,32,128]{2,1,0:T(8,128)S(1)} %get-tuple-element.58), channel_id=1, replica_groups=mesh['x'=4,'y'=8,'c'=2,'z'=8] {'x','y'}, dimensions={0} | all-to-all | bytes 1048576 | tf_op jit(solution)/shard_map/all_to_all | solution.py:33
  131.5 3.0 %shard_map.76 = f32[8,32,128]{2,1,0:T(8,128)S(1)} custom-call(f32[32,32,128]{2,1,0:T(8,128)S(1)} %all_to_all.31.gathered, bf16[1,1024,512]{2,1,0:T(8,128)(2,1)S(1)} %get-tuple-element.59.refs_0_, bf16[1,1024,512]{2,1,0:T(8,128)(2,1)S(1)} %get-tuple-element.60.refs_1_, bf16[2,1024,512]{2,1,0:T(8,128)(2,1)S(1)} %get-tuple-element.61.refs_2_, ...), custom_call_target="tpu_custom_call" | custom-call | flops 1073741824 | bytes 16777216 | tf_op jit(solution)/shard_map/pallas_call | solution.py:264
  134.5 7.3 %collective-permute-start.11 = (f32[8,32,128]{2,1,0:T(8,128)S(1)}, f32[8,32,128]{2,1,0:T(8,128)S(1)}, u32[]{:S(2)}, u32[]{:S(2)}) collective-permute-start(f32[8,32,128]{2,1,0:T(8,128)S(1)} %shard_map.76), channel_id=1, source_target_pairs={{0,8},{8,0},{1,9},{9,1},{2,10},{10,2},{3,11},{11,3},{4,12},{12,4},... | collective-permute-start | bytes 393224 | tf_op jit(solution)/shard_map/ppermute | solution.py:29
  141.8 3.0 %shard_map.75 = f32[8,32,128]{2,1,0:T(8,128)S(1)} custom-call(f32[32,32,128]{2,1,0:T(8,128)S(1)} %all_to_all.31.gathered, bf16[1,1024,512]{2,1,0:T(8,128)(2,1)S(1)} %get-tuple-element.59.refs_0_, bf16[1,1024,512]{2,1,0:T(8,128)(2,1)S(1)} %get-tuple-element.60.refs_1_, bf16[2,1024,512]{2,1,0:T(8,128)(2,1)S(1)} %get-tuple-element.61.refs_2_, ...), custom_call_target="tpu_custom_call" | custom-call | flops 1073741824 | bytes 16777216 | tf_op jit(solution)/shard_map/pallas_call | solution.py:264
  144.8 0.0 collective-permute-done.11
  144.8 11.9 %all_to_all.32.arrived = f32[8,32,128]{2,1,0:T(8,128)S(1)} all-to-all(f32[8,32,128]{2,1,0:T(8,128)S(1)} %add.7), channel_id=1, replica_groups=mesh['x'=4,'y'=8,'c'=2,'z'=8] {'z'}, dimensions={0} | all-to-all | bytes 262144 | tf_op jit(solution)/shard_map/all_to_all | solution.py:33
  156.7 0.2 settle.1
  156.9 11.4 %all_to_all.33 = f32[16,1,128]{2,1,0:T(1,128)S(1)} all-to-all(f32[16,1,128]{2,1,0:T(1,128)S(1)} %broadcast_in_dim.19), channel_id=1, replica_groups=mesh['x'=4,'y'=8,'c'=2,'z'=8] {'y','c'}, dimensions={0} | all-to-all | bytes 16384 | tf_op jit(solution)/shard_map/all_to_all | solution.py:33
  168.3 11.6 %all_to_all.34.sums = f32[32,1,128]{2,1,0:T(1,128)S(1)} all-to-all(f32[32,1,128]{2,1,0:T(1,128)S(1)} %broadcast_in_dim.20), channel_id=1, replica_groups=mesh['x'=4,'y'=8,'c'=2,'z'=8] {'x','z'}, dimensions={0} | all-to-all | bytes 32768 | tf_op jit(solution)/shard_map/all_to_all | solution.py:33
  180.0 1.0 finish.1
  (15 shorter events, 0.2 us)
Async XLA Ops:
  3.8 29.9 %collective-permute-start.6 = (f32[128,128]{1,0:T(8,128)S(1)}, f32[128,128]{1,0:T(8,128)S(1)}, u32[]{:S(2)}, u32[]{:S(2)}) collective-permute-start(f32[128,128]{1,0:T(8,128)S(1)} %get-tuple-element.41.refs_0_), channel_id=1, source_target_pairs={{0,4},{1,5},{2,6},{3,7},{4,0},{5,1},{6,2},{7,3},{8,12},{9,13},{10,... | collective-permute-start | bytes 196616 | tf_op jit(solution)/shard_map/ppermute | solution.py:29
  15.2 12.1 %collective-permute-start.5 = (f32[128,128]{1,0:T(8,128)S(1)}, f32[128,128]{1,0:T(8,128)S(1)}, u32[]{:S(2)}, u32[]{:S(2)}) collective-permute-start(f32[128,128]{1,0:T(8,128)S(1)} %get-tuple-element.41.refs_0_), channel_id=1, source_target_pairs={{0,7},{1,0},{2,1},{3,2},{4,3},{5,4},{6,5},{7,6},{8,15},{9,8},{10,9... | collective-permute-start | bytes 196616 | tf_op jit(solution)/shard_map/ppermute | solution.py:29
  17.2 10.2 %collective-permute-start.4 = (f32[128,128]{1,0:T(8,128)S(1)}, f32[128,128]{1,0:T(8,128)S(1)}, u32[]{:S(2)}, u32[]{:S(2)}) collective-permute-start(f32[128,128]{1,0:T(8,128)S(1)} %get-tuple-element.41.refs_0_), channel_id=1, source_target_pairs={{0,1},{1,2},{2,3},{3,4},{4,5},{5,6},{6,7},{7,0},{8,9},{9,10},{10,1... | collective-permute-start | bytes 196616 | tf_op jit(solution)/shard_map/ppermute | solution.py:29
  20.5 26.1 %all-to-all-start = ((f32[8,160,128]{2,1,0:T(8,128)}), f32[8,160,128]{2,1,0:T(8,128)S(1)}, u32[]{:S(2)}, u32[]{:S(2)}) async-start(f32[8,160,128]{2,1,0:T(8,128)} %get-tuple-element.40), calls=%async_computation | async-start | bytes 1310720 | tf_op jit(solution)/shard_map/all_to_all | solution.py:33
  27.4 10.7 %collective-permute-start.8 = (f32[2,128,128]{2,1,0:T(8,128)S(1)}, f32[2,128,128]{2,1,0:T(8,128)S(1)}, u32[]{:S(2)}, u32[]{:S(2)}) collective-permute-start(f32[2,128,128]{2,1,0:T(8,128)S(1)} %get-tuple-element.76), channel_id=1, source_target_pairs={{0,6},{1,7},{2,0},{3,1},{4,2},{5,3},{6,4},{7,5},{8,14},{9,15},{10,... | collective-permute-start | bytes 393224 | tf_op jit(solution)/shard_map/ppermute | solution.py:29
  29.4 8.8 %collective-permute-start.7 = (f32[2,128,128]{2,1,0:T(8,128)S(1)}, f32[2,128,128]{2,1,0:T(8,128)S(1)}, u32[]{:S(2)}, u32[]{:S(2)}) collective-permute-start(f32[2,128,128]{2,1,0:T(8,128)S(1)} %get-tuple-element.77), channel_id=1, source_target_pairs={{0,2},{1,3},{2,4},{3,5},{4,6},{5,7},{6,0},{7,1},{8,10},{9,11},{10,... | collective-permute-start | bytes 393224 | tf_op jit(solution)/shard_map/ppermute | solution.py:29
  38.2 21.3 %collective-permute-start.9 = (f32[8,128,128]{2,1,0:T(8,128)S(1)}, f32[8,128,128]{2,1,0:T(8,128)S(1)}, u32[]{:S(2)}, u32[]{:S(2)}) collective-permute-start(f32[8,128,128]{2,1,0:T(8,128)S(1)} %constant_dynamic-update-slice_fusion), channel_id=1, source_target_pairs={{0,8},{8,0},{1,9},{9,1},{2,10},{10,2},{3,11},{11,3},{4,12},{12,4},... | collective-permute-start | bytes 1572872 | tf_op jit(solution)/shard_map/ppermute | solution.py:29
  46.6 17.2 %collective-permute-start.2 = (f32[8,160,128]{2,1,0:T(8,128)S(1)}, f32[8,160,128]{2,1,0:T(8,128)S(1)}, u32[]{:S(2)}, u32[]{:S(2)}) collective-permute-start(f32[8,160,128]{2,1,0:T(8,128)S(1)} %all-to-all-done.cols), channel_id=1, source_target_pairs={{0,384},{128,0},{256,128},{384,256},{1,385},{129,1},{257,129},{385... | collective-permute-start | bytes 1966088 | tf_op jit(solution)/shard_map/ppermute | solution.py:29
  51.0 18.1 %collective-permute-start.1 = (f32[8,160,128]{2,1,0:T(8,128)S(1)}, f32[8,160,128]{2,1,0:T(8,128)S(1)}, u32[]{:S(2)}, u32[]{:S(2)}) collective-permute-start(f32[8,160,128]{2,1,0:T(8,128)S(1)} %all-to-all-done.cols), channel_id=1, source_target_pairs={{0,128},{128,256},{256,384},{384,0},{1,129},{129,257},{257,385},{3... | collective-permute-start | bytes 1966088 | tf_op jit(solution)/shard_map/ppermute | solution.py:29
  53.0 27.5 %collective-permute-start = (f32[4,160,128]{2,1,0:T(8,128)S(1)}, f32[4,160,128]{2,1,0:T(8,128)S(1)}, u32[]{:S(2)}, u32[]{:S(2)}) collective-permute-start(f32[4,160,128]{2,1,0:T(8,128)S(1)} %slice.8), channel_id=1, source_target_pairs={{0,256},{128,384},{256,0},{384,128},{1,257},{129,385},{257,1},{385... | collective-permute-start | bytes 983048 | tf_op jit(solution)/shard_map/ppermute | solution.py:29
  69.1 12.0 %collective-permute-start.3 = (f32[4,160,128]{2,1,0:T(8,128)S(1)}, f32[4,160,128]{2,1,0:T(8,128)S(1)}, u32[]{:S(2)}, u32[]{:S(2)}) collective-permute-start(f32[4,160,128]{2,1,0:T(8,128)S(1)} %received.1), channel_id=1, source_target_pairs={{0,128},{1,385},{2,130},{3,387},{4,132},{5,389},{6,134},{7,391},{1... | collective-permute-start | bytes 983048 | tf_op jit(solution)/shard_map/ppermute | solution.py:372
  83.6 26.8 %copy-start = (f32[32,128]{1,0:T(8,128)S(1)}, f32[32,128]{1,0:T(8,128)}, u32[]{:S(2)}) copy-start(f32[32,128]{1,0:T(8,128)} %targets.5) | copy-start | bytes 49156
  83.7 12.2 %collective-permute-start.10 = (f32[8,32,128]{2,1,0:T(8,128)S(1)}, f32[8,32,128]{2,1,0:T(8,128)S(1)}, u32[]{:S(2)}, u32[]{:S(2)}) collective-permute-start(f32[8,32,128]{2,1,0:T(8,128)S(1)} %get-tuple-element.57), channel_id=1, source_target_pairs={{0,8},{8,0},{1,9},{9,1},{2,10},{10,2},{3,11},{11,3},{4,12},{12,4},... | collective-permute-start | bytes 393224 | tf_op jit(solution)/shard_map/ppermute | solution.py:29
  134.5 10.3 %collective-permute-start.11 = (f32[8,32,128]{2,1,0:T(8,128)S(1)}, f32[8,32,128]{2,1,0:T(8,128)S(1)}, u32[]{:S(2)}, u32[]{:S(2)}) collective-permute-start(f32[8,32,128]{2,1,0:T(8,128)S(1)} %shard_map.76), channel_id=1, source_target_pairs={{0,8},{8,0},{1,9},{9,1},{2,10},{10,2},{3,11},{11,3},{4,12},{12,4},... | collective-permute-start | bytes 393224 | tf_op jit(solution)/shard_map/ppermute | solution.py:29

commit v3 on v1

--- a/solution.py
+++ b/solution.py
@@ -148,10 +148,9 @@
             out[to * 4 + local] = piece
 
 
-def more_kernel(tiles, last, count, *refs):
-    cols, refs = refs[:count], refs[count:]
+def more_kernel(tiles, last, cols, *refs):
     lefts, befores, (out, high, low, right, right_sq, vecs) = refs[:6], refs[6:-6], refs[-6:]
-    prepare_cols(cols, right, right_sq, vecs)
+    prepare_cols((cols,), right, right_sq, vecs)
     for to, tile in enumerate(tiles):
         ref, at = WHERE[tile]
         made = make_values(
@@ -204,14 +203,14 @@
 
 def more_chunk(tiles, cols, lefts, befores, last=False):
     return pl.pallas_call(
-        functools.partial(more_kernel, tiles, last, len(cols)),
-        in_specs=[VMEM] * (6 + len(cols) + len(befores)),
+        functools.partial(more_kernel, tiles, last),
+        in_specs=[VMEM] * (7 + len(befores)),
         out_specs=[VMEM] * 3,
         out_shape=made(tiles),
         scratch_shapes=RIGHT,
         compiler_params=PARAMS,
         cost_estimate=made_cost(tiles),
-    )(*cols, *[kept(v) for v in lefts], *[kept(v) for v in befores])
+    )(cols, *[kept(v) for v in lefts], *[kept(v) for v in befores])
 
 
 def total(x):
@@ -236,8 +235,7 @@
     )(aux, arrived, targets)
 
 
-def second_kernel(tiles, gathered, *refs):
-    highs, lows, out, vecs = refs[0:7], refs[7:14], refs[14], refs[15]
+def split_vectors(gathered, vecs):
     place = lax.axis_index("x")
     for chunk in range(4):
         source = lax.rem(place + (0, 3, 1, 2)[chunk], 4) * 8
@@ -246,6 +244,13 @@
             high, low = halves(gathered[source + y])
             vecs[chunk, pl.ds(0, RHS), lanes] = high
             vecs[chunk, pl.ds(RHS, RHS), lanes] = low
+
+
+def second_kernel(tiles, fresh, source, *refs):
+    highs, lows, out = refs[0:7], refs[7:14], refs[14]
+    vecs = refs[15] if fresh else source
+    if fresh:
+        split_vectors(source, vecs)
     for tile in tiles:
         product = jnp.zeros((RHS, TILE), F32)
         for chunk in range(4):
@@ -259,17 +264,17 @@
             out[place_of(tile, local)] = product[:, local * BLK : (local + 1) * BLK]
 
 
-def second(tiles, gathered, highs, lows):
+def second(tiles, fresh, source, highs, lows):
     width = len(tiles) * TILE
-    return pl.pallas_call(
-        functools.partial(second_kernel, tiles),
+    out = [pltpu.VMEM((width // BLK, RHS, BLK), F32), pltpu.VMEM((4, 2 * RHS, WIDE), BF16)]
+    return pl.pallas_call(
+        functools.partial(second_kernel, tiles, fresh),
         in_specs=[VMEM] * (1 + len(highs) + len(lows)),
-        out_specs=VMEM,
-        out_shape=pltpu.VMEM((width // BLK, RHS, BLK), F32),
-        scratch_shapes=[pltpu.VMEM((4, 2 * RHS, WIDE), BF16)],
+        out_specs=[VMEM] * (1 + fresh),
+        out_shape=out[: 1 + fresh],
         compiler_params=PARAMS,
         cost_estimate=cost(2 * width * 4 * WIDE * 128, 4 * width * 4 * WIDE, 0),
-    )(gathered, *[kept(v) for v in highs], *[kept(v) for v in lows])
+    )(source if fresh else kept(source), *[kept(v) for v in highs], *[kept(v) for v in lows])
 
 
 def total(x):
@@ -342,7 +347,7 @@
     near, own, aux = spread(points, lengthscales[None], targets, outputscale, noise)
     near = exchange(near, "y")
     behind, ahead = shift(near, "x", 1), shift(near, "x", -1)
-    across = [shift(behind[:4], "x", 1), shift(ahead[4:], "x", -1)]
+    across = shift(near, "x", 2)
     below, above, far = shift(own, "z", 1), shift(own, "z", -1), shift(own, "z", 4)
     pairs = [shift(jnp.stack([below, own]), "z", 2), shift(jnp.stack([own, above]), "z", -2)]
     prepared = own_cols(near)
@@ -354,7 +359,7 @@
     chunks.append(own_chunk([other], prepared, THEIRS))
     pieces, highs, lows, left, left_sq = [list(part) for part in zip(*chunks)]
     lefts = [*left, *left_sq]
-    for cols in ([behind], [ahead]):
+    for cols in (behind, ahead):
         piece, high, low = more_chunk(ALL, cols, lefts, pieces)
         pieces = [piece]
         highs.append(high)
@@ -367,12 +372,13 @@
     arrived = exchange(mine + theirs, "z")
     first, wide = between(aux, arrived, targets)
     gathered = exchange(wide, ("x", "y"))
-    theirs = shift(second(THEIRS, gathered, highs, lows), "c", 1)
-    mine = second(MINE, gathered, highs, lows)
+    theirs, vecs = second(THEIRS, True, gathered, highs, lows)
+    theirs = shift(theirs, "c", 1)
+    (mine,) = second(MINE, False, vecs, highs, lows)
     arrived = exchange(mine + theirs, "z")
     second_image, dots = settle(aux, arrived, targets, first)
-    sums = jnp.sum(to_each(dots[0:1], "z"), axis=0)
-    return tuple(finish(to_each(sums, ("x", "y", "c")), targets, first, second_image))
+    sums = jnp.sum(to_each(dots[0:1], ("x", "c")), axis=0)
+    return tuple(finish(to_each(sums, ("y", "z")), targets, first, second_image))
 
 
 def solution(mesh):

time: 178 us -> 180 us (1.011)
  waiting for transfers between devices: 13.6 us -> 16.7 us
    ppermute x12 -> x11, waiting for transfers between devices: 9.49 us -> 12.7 us  [shift(): lax.ppermute(value, axis, [(s, (s + steps) % count) for s in range(count)])]
    ppermute x12 -> x11, starting transfers between devices: 53.4 us -> 54.1 us  [shift(): lax.ppermute(value, axis, [(s, (s + steps) % count) for s in range(count)])]
  transfers between devices with their start and end apart: 13 -> 12, of which waited for: 3 -> 4; matrix products, arithmetic and copies ran while one was open for 0% -> 0% of each run, Pallas kernels for 11% -> 11%
where the time goes in v3:
time: 180 us
  blocking collectives  70.9 us (39%)
  starting transfers between devices  61 us (34%)
  Pallas kernels  28.5 us (16%)
  waiting for transfers between devices  16.7 us (9%)
  between operations  2.19 us (1%)
    all_to_all x5, blocking collectives, exchange(): return lax.all_to_all(x, axes, 0, 0, tiled=True)  70.9 us
    ppermute x11, starting transfers between devices, shift(): lax.ppermute(value, axis, [(s, (s + steps) % count) for s in range(count)])  54.1 us
    pallas_call x4, Pallas kernels, more_chunk(): pl.pallas_call(functools.partial(more_kernel, tiles, last), in_specs=[VME...  14.2 us
    ppermute x11, waiting for transfers between devices, shift(): lax.ppermute(value, axis, [(s, (s + steps) % count) for s in range(count)])  12.7 us
    all_to_all x1, starting transfers between devices, exchange(): return lax.all_to_all(x, axes, 0, 0, tiled=True)  6.83 us
    pallas_call x2, Pallas kernels, second(): pl.pallas_call(functools.partial(second_kernel, tiles, fresh), in_specs=[...  5.99 us
    pallas_call x3, Pallas kernels, own_chunk(): pl.pallas_call(functools.partial(own_kernel, len(blocks)), in_specs=[VMEM...  4.77 us
    all_to_all x1, waiting for transfers between devices, exchange(): return lax.all_to_all(x, axes, 0, 0, tiled=True)  4.06 us
  transfers between devices with their start and end apart: 12, of which 4 were waited for; matrix products, arithmetic and copies ran while one was open for 0% of the time, Pallas kernels for 11%

profile of v3, /device:TPU:1, one launch (start us, length us, event | category | flops | bytes accessed | tf_op | source)
XLA Modules:
  0.0 179.5 jit_solution(832996791121772950)
XLA Ops:
  1.9 1.9 %spread.1 = (f32[8,160,128]{2,1,0:T(8,128)}, f32[128,128]{1,0:T(8,128)S(1)}, f32[8,128]{1,0:T(8,128)S(1)}) custom-call(f32[128,128]{1,0:T(8,128)} %points_in.1, f32[1,128]{1,0:T(1,128)} %bitcast.16, f32[32,128]{1,0:T(8,128)} %targets.5, f32[1]{0:T(128)S(6)} %copy.13.scale, f32[1]{0:T(128)S(6)} %copy.14.noise), custom_call_target="tpu_custom_call" | custom-call | tf_op jit(solution)/shard_map/spread/pallas_call | solution.py:68
  3.8 11.5 %collective-permute-start.3 = (f32[128,128]{1,0:T(8,128)S(1)}, f32[128,128]{1,0:T(8,128)S(1)}, u32[]{:S(2)}, u32[]{:S(2)}) collective-permute-start(f32[128,128]{1,0:T(8,128)S(1)} %get-tuple-element.43.refs_0_), channel_id=1, source_target_pairs={{0,4},{1,5},{2,6},{3,7},{4,0},{5,1},{6,2},{7,3},{8,12},{9,13},{10,... | collective-permute-start | bytes 196616 | tf_op jit(solution)/shard_map/ppermute | solution.py:29
  15.2 2.0 %collective-permute-start.2 = (f32[128,128]{1,0:T(8,128)S(1)}, f32[128,128]{1,0:T(8,128)S(1)}, u32[]{:S(2)}, u32[]{:S(2)}) collective-permute-start(f32[128,128]{1,0:T(8,128)S(1)} %get-tuple-element.43.refs_0_), channel_id=1, source_target_pairs={{0,7},{1,0},{2,1},{3,2},{4,3},{5,4},{6,5},{7,6},{8,15},{9,8},{10,9... | collective-permute-start | bytes 196616 | tf_op jit(solution)/shard_map/ppermute | solution.py:29
  17.2 3.3 %collective-permute-start.1 = (f32[128,128]{1,0:T(8,128)S(1)}, f32[128,128]{1,0:T(8,128)S(1)}, u32[]{:S(2)}, u32[]{:S(2)}) collective-permute-start(f32[128,128]{1,0:T(8,128)S(1)} %get-tuple-element.43.refs_0_), channel_id=1, source_target_pairs={{0,1},{1,2},{2,3},{3,4},{4,5},{5,6},{6,7},{7,0},{8,9},{9,10},{10,1... | collective-permute-start | bytes 196616 | tf_op jit(solution)/shard_map/ppermute | solution.py:29
  20.5 6.8 %all-to-all-start = ((f32[8,160,128]{2,1,0:T(8,128)}), f32[8,160,128]{2,1,0:T(8,128)S(1)}, u32[]{:S(2)}, u32[]{:S(2)}) async-start(f32[8,160,128]{2,1,0:T(8,128)} %get-tuple-element.42), calls=%async_computation | async-start | bytes 1310720 | tf_op jit(solution)/shard_map/all_to_all | solution.py:33
  27.4 0.0 collective-permute-done.2.refs_2_
  27.4 0.0 collective-permute-done.1.refs_1_
  27.4 1.9 %collective-permute-start.5 = (f32[2,128,128]{2,1,0:T(8,128)S(1)}, f32[2,128,128]{2,1,0:T(8,128)S(1)}, u32[]{:S(2)}, u32[]{:S(2)}) collective-permute-start(f32[2,128,128]{2,1,0:T(8,128)S(1)} %get-tuple-element.80), channel_id=1, source_target_pairs={{0,6},{1,7},{2,0},{3,1},{4,2},{5,3},{6,4},{7,5},{8,14},{9,15},{10,... | collective-permute-start | bytes 393224 | tf_op jit(solution)/shard_map/ppermute | solution.py:29
  29.4 4.2 %collective-permute-start.4 = (f32[2,128,128]{2,1,0:T(8,128)S(1)}, f32[2,128,128]{2,1,0:T(8,128)S(1)}, u32[]{:S(2)}, u32[]{:S(2)}) collective-permute-start(f32[2,128,128]{2,1,0:T(8,128)S(1)} %get-tuple-element.81), channel_id=1, source_target_pairs={{0,2},{1,3},{2,4},{3,5},{4,6},{5,7},{6,0},{7,1},{8,10},{9,11},{10,... | collective-permute-start | bytes 393224 | tf_op jit(solution)/shard_map/ppermute | solution.py:29
  33.7 0.0 collective-permute-done.3.refs_3_
  33.7 4.5 %collective-permute-done.4.refs_0_ = f32[2,128,128]{2,1,0:T(8,128)S(1)} collective-permute-done((f32[2,128,128]{2,1,0:T(8,128)S(1)}, f32[2,128,128]{2,1,0:T(8,128)S(1)}, u32[]{:S(2)}, u32[]{:S(2)}) %collective-permute-start.4) | collective-permute-done | bytes 131104 | tf_op jit(solution)/shard_map/ppermute | solution.py:29
  38.2 0.0 collective-permute-done.5.refs_1_
  38.2 4.4 %collective-permute-start.6 = (f32[8,128,128]{2,1,0:T(8,128)S(1)}, f32[8,128,128]{2,1,0:T(8,128)S(1)}, u32[]{:S(2)}, u32[]{:S(2)}) collective-permute-start(f32[8,128,128]{2,1,0:T(8,128)S(1)} %constant_dynamic-update-slice_fusion), channel_id=1, source_target_pairs={{0,8},{8,0},{1,9},{9,1},{2,10},{10,2},{3,11},{11,3},{4,12},{12,4},... | collective-permute-start | bytes 1572872 | tf_op jit(solution)/shard_map/ppermute | solution.py:29
  42.6 4.1 %all-to-all-done.cols = f32[8,160,128]{2,1,0:T(8,128)S(1)} async-done(((f32[8,160,128]{2,1,0:T(8,128)}), f32[8,160,128]{2,1,0:T(8,128)S(1)}, u32[]{:S(2)}, u32[]{:S(2)}) %all-to-all-start) | async-done | bytes 655392 | tf_op jit(solution)/shard_map/all_to_all | solution.py:33
  46.6 3.1 %collective-permute-start.8 = (f32[8,160,128]{2,1,0:T(8,128)S(1)}, f32[8,160,128]{2,1,0:T(8,128)S(1)}, u32[]{:S(2)}, u32[]{:S(2)}) collective-permute-start(f32[8,160,128]{2,1,0:T(8,128)S(1)} %all-to-all-done.cols), channel_id=1, source_target_pairs={{0,128},{128,256},{256,384},{384,0},{1,129},{129,257},{257,385},{3... | collective-permute-start | bytes 1966088 | tf_op jit(solution)/shard_map/ppermute | solution.py:29
  49.8 3.4 %collective-permute-start.7 = (f32[8,160,128]{2,1,0:T(8,128)S(1)}, f32[8,160,128]{2,1,0:T(8,128)S(1)}, u32[]{:S(2)}, u32[]{:S(2)}) collective-permute-start(f32[8,160,128]{2,1,0:T(8,128)S(1)} %all-to-all-done.cols), channel_id=1, source_target_pairs={{0,384},{128,0},{256,128},{384,256},{1,385},{129,1},{257,129},{385... | collective-permute-start | bytes 1966088 | tf_op jit(solution)/shard_map/ppermute | solution.py:29
  53.1 3.4 %collective-permute-start = (f32[8,160,128]{2,1,0:T(8,128)S(1)}, f32[8,160,128]{2,1,0:T(8,128)S(1)}, u32[]{:S(2)}, u32[]{:S(2)}) collective-permute-start(f32[8,160,128]{2,1,0:T(8,128)S(1)} %all-to-all-done.cols), channel_id=1, source_target_pairs={{0,256},{128,384},{256,0},{384,128},{1,257},{129,385},{257,1},{385... | collective-permute-start | bytes 1966088 | tf_op jit(solution)/shard_map/ppermute | solution.py:29
  56.6 0.4 own_cols.1
  57.0 1.2 shard_map.69
  58.2 0.0 collective-permute-done.6.refs_0_
  58.2 2.3 %shard_map.70 = (f32[8,32,128]{2,1,0:T(8,128)S(1)}, bf16[2,1024,512]{2,1,0:T(8,128)(2,1)S(1)}, bf16[2,1024,512]{2,1,0:T(8,128)(2,1)S(1)}, bf16[2,512,512]{2,1,0:T(8,128)(2,1)S(1)}, f32[2,1,512]{2,1,0:T(1,128)S(1)}) custom-call(f32[8,128,128]{2,1,0:T(8,128)S(1)} %collective-permute-done.6.refs_0_, ...), custom_call_target="tpu_custom_call" | custom-call | flops 1610612736 | bytes 4194304 | tf_op jit(solution)/shard_map/pallas_call | solution.py:194
  60.5 1.2 shard_map.68
  61.8 2.3 %collective-permute-done.8.cols = f32[8,160,128]{2,1,0:T(8,128)S(1)} collective-permute-done((f32[8,160,128]{2,1,0:T(8,128)S(1)}, f32[8,160,128]{2,1,0:T(8,128)S(1)}, u32[]{:S(2)}, u32[]{:S(2)}) %collective-permute-start.8) | collective-permute-done | bytes 655392 | tf_op jit(solution)/shard_map/ppermute | solution.py:29
  64.0 4.5 %shard_map.71 = (f32[16,32,128]{2,1,0:T(8,128)S(1)}, bf16[4,1024,512]{2,1,0:T(8,128)(2,1)S(1)}, bf16[4,1024,512]{2,1,0:T(8,128)(2,1)S(1)}) custom-call(f32[8,160,128]{2,1,0:T(8,128)S(1)} %collective-permute-done.8.cols, bf16[1,512,512]{2,1,0:T(8,128)(2,1)S(1)} %get-tuple-element.47.refs_0_, bf16[1,512,512]{2,1,0:T(8,128)(2,1)S(1)} %get-tuple-element.48.refs_1_, ...), custom_call_target="tpu_custom_call" | custom-call | flops 3221225472 | bytes 8388608 | tf_op jit(solution)/shard_map/pallas_call | solution.py:205
  68.5 0.0 collective-permute-done.7.cols
  68.5 4.6 %shard_map.72 = (f32[16,32,128]{2,1,0:T(8,128)S(1)}, bf16[4,1024,512]{2,1,0:T(8,128)(2,1)S(1)}, bf16[4,1024,512]{2,1,0:T(8,128)(2,1)S(1)}) custom-call(f32[8,160,128]{2,1,0:T(8,128)S(1)} %collective-permute-done.7.cols, bf16[1,512,512]{2,1,0:T(8,128)(2,1)S(1)} %get-tuple-element.47.refs_0_, bf16[1,512,512]{2,1,0:T(8,128)(2,1)S(1)} %get-tuple-element.48.refs_1_, ...), custom_call_target="tpu_custom_call" | custom-call | flops 3221225472 | bytes 8388608 | tf_op jit(solution)/shard_map/pallas_call | solution.py:205
  73.1 5.9 %collective-permute-done.cols = f32[8,160,128]{2,1,0:T(8,128)S(1)} collective-permute-done((f32[8,160,128]{2,1,0:T(8,128)S(1)}, f32[8,160,128]{2,1,0:T(8,128)S(1)}, u32[]{:S(2)}, u32[]{:S(2)}) %collective-permute-start) | collective-permute-done | bytes 655392 | tf_op jit(solution)/shard_map/ppermute | solution.py:29
  79.0 2.7 %shard_map.74 = (f32[8,32,128]{2,1,0:T(8,128)S(1)}, bf16[2,1024,512]{2,1,0:T(8,128)(2,1)S(1)}, bf16[2,1024,512]{2,1,0:T(8,128)(2,1)S(1)}) custom-call(f32[8,160,128]{2,1,0:T(8,128)S(1)} %collective-permute-done.cols, bf16[1,512,512]{2,1,0:T(8,128)(2,1)S(1)} %get-tuple-element.47.refs_0_, bf16[1,512,512]{2,1,0:T(8,128)(2,1)S(1)} %get-tuple-element.48.refs_1_, ...), custom_call_target="tpu_custom_call" | custom-call | flops 1610612736 | bytes 4194304 | tf_op jit(solution)/shard_map/pallas_call | solution.py:205
  81.8 0.0 copy-start
  81.8 9.6 %collective-permute-start.9 = (f32[8,32,128]{2,1,0:T(8,128)S(1)}, f32[8,32,128]{2,1,0:T(8,128)S(1)}, u32[]{:S(2)}, u32[]{:S(2)}) collective-permute-start(f32[8,32,128]{2,1,0:T(8,128)S(1)} %get-tuple-element.59), channel_id=1, source_target_pairs={{0,8},{8,0},{1,9},{9,1},{2,10},{10,2},{3,11},{11,3},{4,12},{12,4},... | collective-permute-start | bytes 393224 | tf_op jit(solution)/shard_map/ppermute | solution.py:29
  91.4 2.4 %shard_map.73 = (f32[8,32,128]{2,1,0:T(8,128)S(1)}, bf16[2,1024,512]{2,1,0:T(8,128)(2,1)S(1)}, bf16[2,1024,512]{2,1,0:T(8,128)(2,1)S(1)}) custom-call(f32[8,160,128]{2,1,0:T(8,128)S(1)} %collective-permute-done.cols, bf16[1,512,512]{2,1,0:T(8,128)(2,1)S(1)} %get-tuple-element.47.refs_0_, bf16[1,512,512]{2,1,0:T(8,128)(2,1)S(1)} %get-tuple-element.48.refs_1_, ...), custom_call_target="tpu_custom_call" | custom-call | flops 1610612736 | bytes 4194304 | tf_op jit(solution)/shard_map/pallas_call | solution.py:205
  93.8 0.0 collective-permute-done.9
  93.9 14.0 %all_to_all.30.arrived = f32[8,32,128]{2,1,0:T(8,128)S(1)} all-to-all(f32[8,32,128]{2,1,0:T(8,128)S(1)} %add.6), channel_id=1, replica_groups=mesh['x'=4,'y'=8,'c'=2,'z'=8] {'z'}, dimensions={0} | all-to-all | bytes 262144 | tf_op jit(solution)/shard_map/all_to_all | solution.py:33
  107.8 0.0 copy-done
  107.8 0.1 between.1
  107.9 22.2 %all_to_all.31.source = f32[32,32,128]{2,1,0:T(8,128)S(1)} all-to-all(f32[32,32,128]{2,1,0:T(8,128)S(1)} %get-tuple-element.60), channel_id=1, replica_groups=mesh['x'=4,'y'=8,'c'=2,'z'=8] {'x','y'}, dimensions={0} | all-to-all | bytes 1048576 | tf_op jit(solution)/shard_map/all_to_all | solution.py:33
  130.1 3.0 %shard_map.75 = (f32[8,32,128]{2,1,0:T(8,128)S(1)}, bf16[4,64,1024]{2,1,0:T(8,128)(2,1)S(1)}) custom-call(f32[32,32,128]{2,1,0:T(8,128)S(1)} %all_to_all.31.source, bf16[1,1024,512]{2,1,0:T(8,128)(2,1)S(1)} %get-tuple-element.61.refs_0_, bf16[1,1024,512]{2,1,0:T(8,128)(2,1)S(1)} %get-tuple-element.62.refs_1_, ...), custom_call_target="tpu_custom_call" | custom-call | flops 1073741824 | bytes 16777216 | tf_op jit(solution)/shard_map/pallas_call | solution.py:270
  133.1 7.3 %collective-permute-start.10 = (f32[8,32,128]{2,1,0:T(8,128)S(1)}, f32[8,32,128]{2,1,0:T(8,128)S(1)}, u32[]{:S(2)}, u32[]{:S(2)}) collective-permute-start(f32[8,32,128]{2,1,0:T(8,128)S(1)} %get-tuple-element.76), channel_id=1, source_target_pairs={{0,8},{8,0},{1,9},{9,1},{2,10},{10,2},{3,11},{11,3},{4,12},{12,4},... | collective-permute-start | bytes 393224 | tf_op jit(solution)/shard_map/ppermute | solution.py:29
  140.4 3.0 %shard_map.76 = f32[8,32,128]{2,1,0:T(8,128)S(1)} custom-call(bf16[4,64,1024]{2,1,0:T(8,128)(2,1)S(1)} %get-tuple-element.75.source, bf16[1,1024,512]{2,1,0:T(8,128)(2,1)S(1)} %get-tuple-element.61.refs_0_, bf16[1,1024,512]{2,1,0:T(8,128)(2,1)S(1)} %get-tuple-element.62.refs_1_, bf16[2,1024,512]{2,1,0:T(8,128)(2,1)S(1)} %get-tuple-element.63.refs_2_, ...), custom_call_target="tpu_custom_call" | custom-call | flops 1073741824 | bytes 16777216 | tf_op jit(solution)/shard_map/pallas_call | solution.py:270
  143.4 0.0 collective-permute-done.10
  143.4 11.9 %all_to_all.32.arrived = f32[8,32,128]{2,1,0:T(8,128)S(1)} all-to-all(f32[8,32,128]{2,1,0:T(8,128)S(1)} %add.7), channel_id=1, replica_groups=mesh['x'=4,'y'=8,'c'=2,'z'=8] {'z'}, dimensions={0} | all-to-all | bytes 262144 | tf_op jit(solution)/shard_map/all_to_all | solution.py:33
  155.3 0.2 settle.1
  155.5 7.5 %all_to_all.33 = f32[8,1,128]{2,1,0:T(1,128)S(1)} all-to-all(f32[8,1,128]{2,1,0:T(1,128)S(1)} %broadcast_in_dim.19), channel_id=1, replica_groups=mesh['x'=4,'y'=8,'c'=2,'z'=8] {'x','c'}, dimensions={0} | all-to-all | bytes 8192 | tf_op jit(solution)/shard_map/all_to_all | solution.py:33
  163.1 15.5 %all_to_all.34.sums = f32[64,1,128]{2,1,0:T(1,128)S(1)} all-to-all(f32[64,1,128]{2,1,0:T(1,128)S(1)} %broadcast_in_dim.20), channel_id=1, replica_groups=mesh['x'=4,'y'=8,'c'=2,'z'=8] {'y','z'}, dimensions={0} | all-to-all | bytes 65536 | tf_op jit(solution)/shard_map/all_to_all | solution.py:33
  178.5 1.0 finish.1
  (13 shorter events, 0.2 us)
Async XLA Ops:
  3.8 29.9 %collective-permute-start.3 = (f32[128,128]{1,0:T(8,128)S(1)}, f32[128,128]{1,0:T(8,128)S(1)}, u32[]{:S(2)}, u32[]{:S(2)}) collective-permute-start(f32[128,128]{1,0:T(8,128)S(1)} %get-tuple-element.43.refs_0_), channel_id=1, source_target_pairs={{0,4},{1,5},{2,6},{3,7},{4,0},{5,1},{6,2},{7,3},{8,12},{9,13},{10,... | collective-permute-start | bytes 196616 | tf_op jit(solution)/shard_map/ppermute | solution.py:29
  15.2 12.1 %collective-permute-start.2 = (f32[128,128]{1,0:T(8,128)S(1)}, f32[128,128]{1,0:T(8,128)S(1)}, u32[]{:S(2)}, u32[]{:S(2)}) collective-permute-start(f32[128,128]{1,0:T(8,128)S(1)} %get-tuple-element.43.refs_0_), channel_id=1, source_target_pairs={{0,7},{1,0},{2,1},{3,2},{4,3},{5,4},{6,5},{7,6},{8,15},{9,8},{10,9... | collective-permute-start | bytes 196616 | tf_op jit(solution)/shard_map/ppermute | solution.py:29
  17.2 10.2 %collective-permute-start.1 = (f32[128,128]{1,0:T(8,128)S(1)}, f32[128,128]{1,0:T(8,128)S(1)}, u32[]{:S(2)}, u32[]{:S(2)}) collective-permute-start(f32[128,128]{1,0:T(8,128)S(1)} %get-tuple-element.43.refs_0_), channel_id=1, source_target_pairs={{0,1},{1,2},{2,3},{3,4},{4,5},{5,6},{6,7},{7,0},{8,9},{9,10},{10,1... | collective-permute-start | bytes 196616 | tf_op jit(solution)/shard_map/ppermute | solution.py:29
  20.5 26.1 %all-to-all-start = ((f32[8,160,128]{2,1,0:T(8,128)}), f32[8,160,128]{2,1,0:T(8,128)S(1)}, u32[]{:S(2)}, u32[]{:S(2)}) async-start(f32[8,160,128]{2,1,0:T(8,128)} %get-tuple-element.42), calls=%async_computation | async-start | bytes 1310720 | tf_op jit(solution)/shard_map/all_to_all | solution.py:33
  27.4 10.7 %collective-permute-start.5 = (f32[2,128,128]{2,1,0:T(8,128)S(1)}, f32[2,128,128]{2,1,0:T(8,128)S(1)}, u32[]{:S(2)}, u32[]{:S(2)}) collective-permute-start(f32[2,128,128]{2,1,0:T(8,128)S(1)} %get-tuple-element.80), channel_id=1, source_target_pairs={{0,6},{1,7},{2,0},{3,1},{4,2},{5,3},{6,4},{7,5},{8,14},{9,15},{10,... | collective-permute-start | bytes 393224 | tf_op jit(solution)/shard_map/ppermute | solution.py:29
  29.4 8.8 %collective-permute-start.4 = (f32[2,128,128]{2,1,0:T(8,128)S(1)}, f32[2,128,128]{2,1,0:T(8,128)S(1)}, u32[]{:S(2)}, u32[]{:S(2)}) collective-permute-start(f32[2,128,128]{2,1,0:T(8,128)S(1)} %get-tuple-element.81), channel_id=1, source_target_pairs={{0,2},{1,3},{2,4},{3,5},{4,6},{5,7},{6,0},{7,1},{8,10},{9,11},{10,... | collective-permute-start | bytes 393224 | tf_op jit(solution)/shard_map/ppermute | solution.py:29
  38.2 20.0 %collective-permute-start.6 = (f32[8,128,128]{2,1,0:T(8,128)S(1)}, f32[8,128,128]{2,1,0:T(8,128)S(1)}, u32[]{:S(2)}, u32[]{:S(2)}) collective-permute-start(f32[8,128,128]{2,1,0:T(8,128)S(1)} %constant_dynamic-update-slice_fusion), channel_id=1, source_target_pairs={{0,8},{8,0},{1,9},{9,1},{2,10},{10,2},{3,11},{11,3},{4,12},{12,4},... | collective-permute-start | bytes 1572872 | tf_op jit(solution)/shard_map/ppermute | solution.py:29
  46.6 17.4 %collective-permute-start.8 = (f32[8,160,128]{2,1,0:T(8,128)S(1)}, f32[8,160,128]{2,1,0:T(8,128)S(1)}, u32[]{:S(2)}, u32[]{:S(2)}) collective-permute-start(f32[8,160,128]{2,1,0:T(8,128)S(1)} %all-to-all-done.cols), channel_id=1, source_target_pairs={{0,128},{128,256},{256,384},{384,0},{1,129},{129,257},{257,385},{3... | collective-permute-start | bytes 1966088 | tf_op jit(solution)/shard_map/ppermute | solution.py:29
  49.8 18.7 %collective-permute-start.7 = (f32[8,160,128]{2,1,0:T(8,128)S(1)}, f32[8,160,128]{2,1,0:T(8,128)S(1)}, u32[]{:S(2)}, u32[]{:S(2)}) collective-permute-start(f32[8,160,128]{2,1,0:T(8,128)S(1)} %all-to-all-done.cols), channel_id=1, source_target_pairs={{0,384},{128,0},{256,128},{384,256},{1,385},{129,1},{257,129},{385... | collective-permute-start | bytes 1966088 | tf_op jit(solution)/shard_map/ppermute | solution.py:29
  53.1 25.9 %collective-permute-start = (f32[8,160,128]{2,1,0:T(8,128)S(1)}, f32[8,160,128]{2,1,0:T(8,128)S(1)}, u32[]{:S(2)}, u32[]{:S(2)}) collective-permute-start(f32[8,160,128]{2,1,0:T(8,128)S(1)} %all-to-all-done.cols), channel_id=1, source_target_pairs={{0,256},{128,384},{256,0},{384,128},{1,257},{129,385},{257,1},{385... | collective-permute-start | bytes 1966088 | tf_op jit(solution)/shard_map/ppermute | solution.py:29
  81.8 26.1 %copy-start = (f32[32,128]{1,0:T(8,128)S(1)}, f32[32,128]{1,0:T(8,128)}, u32[]{:S(2)}) copy-start(f32[32,128]{1,0:T(8,128)} %targets.5) | copy-start | bytes 49156
  81.8 12.1 %collective-permute-start.9 = (f32[8,32,128]{2,1,0:T(8,128)S(1)}, f32[8,32,128]{2,1,0:T(8,128)S(1)}, u32[]{:S(2)}, u32[]{:S(2)}) collective-permute-start(f32[8,32,128]{2,1,0:T(8,128)S(1)} %get-tuple-element.59), channel_id=1, source_target_pairs={{0,8},{8,0},{1,9},{9,1},{2,10},{10,2},{3,11},{11,3},{4,12},{12,4},... | collective-permute-start | bytes 393224 | tf_op jit(solution)/shard_map/ppermute | solution.py:29
  133.1 10.3 %collective-permute-start.10 = (f32[8,32,128]{2,1,0:T(8,128)S(1)}, f32[8,32,128]{2,1,0:T(8,128)S(1)}, u32[]{:S(2)}, u32[]{:S(2)}) collective-permute-start(f32[8,32,128]{2,1,0:T(8,128)S(1)} %get-tuple-element.76), channel_id=1, source_target_pairs={{0,8},{8,0},{1,9},{9,1},{2,10},{10,2},{3,11},{11,3},{4,12},{12,4},... | collective-permute-start | bytes 393224 | tf_op jit(solution)/shard_map/ppermute | solution.py:29

commit v4 on v0

--- a/solution.py
+++ b/solution.py
@@ -148,10 +148,9 @@
             out[to * 4 + local] = piece
 
 
-def more_kernel(tiles, last, *refs):
-    cols, refs = refs[:2], refs[2:]
+def more_kernel(tiles, last, cols, *refs):
     lefts, befores, (out, high, low, right, right_sq, vecs) = refs[:6], refs[6:-6], refs[-6:]
-    prepare_cols(cols, right, right_sq, vecs)
+    prepare_cols((cols,), right, right_sq, vecs)
     for to, tile in enumerate(tiles):
         ref, at = WHERE[tile]
         made = make_values(
@@ -205,13 +204,13 @@
 def more_chunk(tiles, cols, lefts, befores, last=False):
     return pl.pallas_call(
         functools.partial(more_kernel, tiles, last),
-        in_specs=[VMEM] * (8 + len(befores)),
+        in_specs=[VMEM] * (7 + len(befores)),
         out_specs=[VMEM] * 3,
         out_shape=made(tiles),
         scratch_shapes=RIGHT,
         compiler_params=PARAMS,
         cost_estimate=made_cost(tiles),
-    )(*cols, *[kept(v) for v in lefts], *[kept(v) for v in befores])
+    )(cols, *[kept(v) for v in lefts], *[kept(v) for v in befores])
 
 
 def total(x):
@@ -341,9 +340,9 @@
 def on_device(points, targets, lengthscales, outputscale, noise):
     near, own, aux = spread(points, lengthscales[None], targets, outputscale, noise)
     near = exchange(near, "y")
-    behind_low, ahead_high = shift(near[:4], "x", 1), shift(near[4:], "x", -1)
-    behind_high, ahead_low = shift(near[4:], "x", 1), shift(near[:4], "x", -1)
-    across = [shift(behind_low, "x", 1), shift(ahead_high, "x", -1)]
+    ahead = shift(near, "x", -1)
+    behind = shift(near, "x", 1)
+    across = shift(near, "x", 2)
     below, above, far = shift(own, "z", 1), shift(own, "z", -1), shift(own, "z", 4)
     pairs = [shift(jnp.stack([below, own]), "z", 2), shift(jnp.stack([own, above]), "z", -2)]
     prepared = own_cols(near)
@@ -355,7 +354,7 @@
     chunks.append(own_chunk([other], prepared, THEIRS))
     pieces, highs, lows, left, left_sq = [list(part) for part in zip(*chunks)]
     lefts = [*left, *left_sq]
-    for cols in ([behind_low, behind_high], [ahead_low, ahead_high]):
+    for cols in (behind, ahead):
         piece, high, low = more_chunk(ALL, cols, lefts, pieces)
         pieces = [piece]
         highs.append(high)

time: 173 us -> 180 us (1.040)
  waiting for transfers between devices: 8.57 us -> 16.8 us
  starting transfers between devices: 65 us -> 61 us
  blocking collectives: 68.5 us -> 70.9 us
    ppermute x14 -> x11, waiting for transfers between devices: 4.51 us -> 12.8 us  [shift(): lax.ppermute(value, axis, [(s, (s + steps) % count) for s in range(count)])]
    ppermute x14 -> x11, starting transfers between devices: 58.1 us -> 54.1 us  [shift(): lax.ppermute(value, axis, [(s, (s + steps) % count) for s in range(count)])]
    all_to_all x5, blocking collectives: 68.5 us -> 70.9 us  [exchange(): return lax.all_to_all(x, axes, 0, 0, tiled=True)]
  transfers between devices with their start and end apart: 15 -> 12, of which waited for: 2 -> 4; matrix products, arithmetic and copies ran while one was open for 0% -> 0% of each run, Pallas kernels for 11% -> 11%
where the time goes in v4:
time: 180 us; the launch traced here: 179 us
  blocking collectives  70.9 us (39%)
  starting transfers between devices  61 us (34%)
  Pallas kernels  28.4 us (16%)
  waiting for transfers between devices  16.8 us (9%)
  between operations  2.19 us (1%)
    all_to_all x5, blocking collectives, exchange(): return lax.all_to_all(x, axes, 0, 0, tiled=True)  70.9 us
    ppermute x11, starting transfers between devices, shift(): lax.ppermute(value, axis, [(s, (s + steps) % count) for s in range(count)])  54.1 us
    pallas_call x4, Pallas kernels, more_chunk(): pl.pallas_call(functools.partial(more_kernel, tiles, last), in_specs=[VME...  14.1 us
    ppermute x11, waiting for transfers between devices, shift(): lax.ppermute(value, axis, [(s, (s + steps) % count) for s in range(count)])  12.8 us
    all_to_all x1, starting transfers between devices, exchange(): return lax.all_to_all(x, axes, 0, 0, tiled=True)  6.83 us
    pallas_call x2, Pallas kernels, second(): pl.pallas_call(functools.partial(second_kernel, tiles), in_specs=[VMEM] *...  6.01 us
    pallas_call x3, Pallas kernels, own_chunk(): pl.pallas_call(functools.partial(own_kernel, len(blocks)), in_specs=[VMEM...  4.7 us
    all_to_all x1, waiting for transfers between devices, exchange(): return lax.all_to_all(x, axes, 0, 0, tiled=True)  4.06 us
  transfers between devices with their start and end apart: 12, of which 4 were waited for; matrix products, arithmetic and copies ran while one was open for 0% of the time, Pallas kernels for 11%

profile of v4, /device:TPU:1, one launch (start us, length us, event | category | flops | bytes accessed | tf_op | source)
XLA Modules:
  0.0 179.5 jit_solution(6721750555901534543)
XLA Ops:
  1.9 1.9 %spread.1 = (f32[8,160,128]{2,1,0:T(8,128)}, f32[128,128]{1,0:T(8,128)S(1)}, f32[8,128]{1,0:T(8,128)S(1)}) custom-call(f32[128,128]{1,0:T(8,128)} %points_in.1, f32[1,128]{1,0:T(1,128)} %bitcast.16, f32[32,128]{1,0:T(8,128)} %targets.5, f32[1]{0:T(128)S(6)} %copy.13.scale, f32[1]{0:T(128)S(6)} %copy.14.noise), custom_call_target="tpu_custom_call" | custom-call | tf_op jit(solution)/shard_map/spread/pallas_call | solution.py:68
  3.8 11.5 %collective-permute-start.3 = (f32[128,128]{1,0:T(8,128)S(1)}, f32[128,128]{1,0:T(8,128)S(1)}, u32[]{:S(2)}, u32[]{:S(2)}) collective-permute-start(f32[128,128]{1,0:T(8,128)S(1)} %get-tuple-element.41.refs_0_), channel_id=1, source_target_pairs={{0,4},{1,5},{2,6},{3,7},{4,0},{5,1},{6,2},{7,3},{8,12},{9,13},{10,... | collective-permute-start | bytes 196616 | tf_op jit(solution)/shard_map/ppermute | solution.py:29
  15.3 2.0 %collective-permute-start.2 = (f32[128,128]{1,0:T(8,128)S(1)}, f32[128,128]{1,0:T(8,128)S(1)}, u32[]{:S(2)}, u32[]{:S(2)}) collective-permute-start(f32[128,128]{1,0:T(8,128)S(1)} %get-tuple-element.41.refs_0_), channel_id=1, source_target_pairs={{0,7},{1,0},{2,1},{3,2},{4,3},{5,4},{6,5},{7,6},{8,15},{9,8},{10,9... | collective-permute-start | bytes 196616 | tf_op jit(solution)/shard_map/ppermute | solution.py:29
  17.2 3.3 %collective-permute-start.1 = (f32[128,128]{1,0:T(8,128)S(1)}, f32[128,128]{1,0:T(8,128)S(1)}, u32[]{:S(2)}, u32[]{:S(2)}) collective-permute-start(f32[128,128]{1,0:T(8,128)S(1)} %get-tuple-element.41.refs_0_), channel_id=1, source_target_pairs={{0,1},{1,2},{2,3},{3,4},{4,5},{5,6},{6,7},{7,0},{8,9},{9,10},{10,1... | collective-permute-start | bytes 196616 | tf_op jit(solution)/shard_map/ppermute | solution.py:29
  20.6 6.8 %all-to-all-start = ((f32[8,160,128]{2,1,0:T(8,128)}), f32[8,160,128]{2,1,0:T(8,128)S(1)}, u32[]{:S(2)}, u32[]{:S(2)}) async-start(f32[8,160,128]{2,1,0:T(8,128)} %get-tuple-element.40), calls=%async_computation | async-start | bytes 1310720 | tf_op jit(solution)/shard_map/all_to_all | solution.py:33
  27.4 0.0 collective-permute-done.2.refs_2_
  27.4 0.0 collective-permute-done.1.refs_1_
  27.4 1.9 %collective-permute-start.5 = (f32[2,128,128]{2,1,0:T(8,128)S(1)}, f32[2,128,128]{2,1,0:T(8,128)S(1)}, u32[]{:S(2)}, u32[]{:S(2)}) collective-permute-start(f32[2,128,128]{2,1,0:T(8,128)S(1)} %get-tuple-element.76), channel_id=1, source_target_pairs={{0,6},{1,7},{2,0},{3,1},{4,2},{5,3},{6,4},{7,5},{8,14},{9,15},{10,... | collective-permute-start | bytes 393224 | tf_op jit(solution)/shard_map/ppermute | solution.py:29
  29.4 4.2 %collective-permute-start.4 = (f32[2,128,128]{2,1,0:T(8,128)S(1)}, f32[2,128,128]{2,1,0:T(8,128)S(1)}, u32[]{:S(2)}, u32[]{:S(2)}) collective-permute-start(f32[2,128,128]{2,1,0:T(8,128)S(1)} %get-tuple-element.77), channel_id=1, source_target_pairs={{0,2},{1,3},{2,4},{3,5},{4,6},{5,7},{6,0},{7,1},{8,10},{9,11},{10,... | collective-permute-start | bytes 393224 | tf_op jit(solution)/shard_map/ppermute | solution.py:29
  33.7 0.0 collective-permute-done.3.refs_3_
  33.7 4.5 %collective-permute-done.4.refs_0_ = f32[2,128,128]{2,1,0:T(8,128)S(1)} collective-permute-done((f32[2,128,128]{2,1,0:T(8,128)S(1)}, f32[2,128,128]{2,1,0:T(8,128)S(1)}, u32[]{:S(2)}, u32[]{:S(2)}) %collective-permute-start.4) | collective-permute-done | bytes 131104 | tf_op jit(solution)/shard_map/ppermute | solution.py:29
  38.2 0.0 collective-permute-done.5.refs_1_
  38.2 4.4 %collective-permute-start.6 = (f32[8,128,128]{2,1,0:T(8,128)S(1)}, f32[8,128,128]{2,1,0:T(8,128)S(1)}, u32[]{:S(2)}, u32[]{:S(2)}) collective-permute-start(f32[8,128,128]{2,1,0:T(8,128)S(1)} %constant_dynamic-update-slice_fusion), channel_id=1, source_target_pairs={{0,8},{8,0},{1,9},{9,1},{2,10},{10,2},{3,11},{11,3},{4,12},{12,4},... | collective-permute-start | bytes 1572872 | tf_op jit(solution)/shard_map/ppermute | solution.py:29
  42.6 4.1 %all-to-all-done.cols = f32[8,160,128]{2,1,0:T(8,128)S(1)} async-done(((f32[8,160,128]{2,1,0:T(8,128)}), f32[8,160,128]{2,1,0:T(8,128)S(1)}, u32[]{:S(2)}, u32[]{:S(2)}) %all-to-all-start) | async-done | bytes 655392 | tf_op jit(solution)/shard_map/all_to_all | solution.py:33
  46.6 3.1 %collective-permute-start.8 = (f32[8,160,128]{2,1,0:T(8,128)S(1)}, f32[8,160,128]{2,1,0:T(8,128)S(1)}, u32[]{:S(2)}, u32[]{:S(2)}) collective-permute-start(f32[8,160,128]{2,1,0:T(8,128)S(1)} %all-to-all-done.cols), channel_id=1, source_target_pairs={{0,128},{128,256},{256,384},{384,0},{1,129},{129,257},{257,385},{3... | collective-permute-start | bytes 1966088 | tf_op jit(solution)/shard_map/ppermute | solution.py:29
  49.8 3.4 %collective-permute-start.7 = (f32[8,160,128]{2,1,0:T(8,128)S(1)}, f32[8,160,128]{2,1,0:T(8,128)S(1)}, u32[]{:S(2)}, u32[]{:S(2)}) collective-permute-start(f32[8,160,128]{2,1,0:T(8,128)S(1)} %all-to-all-done.cols), channel_id=1, source_target_pairs={{0,384},{128,0},{256,128},{384,256},{1,385},{129,1},{257,129},{385... | collective-permute-start | bytes 1966088 | tf_op jit(solution)/shard_map/ppermute | solution.py:29
  53.1 3.4 %collective-permute-start = (f32[8,160,128]{2,1,0:T(8,128)S(1)}, f32[8,160,128]{2,1,0:T(8,128)S(1)}, u32[]{:S(2)}, u32[]{:S(2)}) collective-permute-start(f32[8,160,128]{2,1,0:T(8,128)S(1)} %all-to-all-done.cols), channel_id=1, source_target_pairs={{0,256},{128,384},{256,0},{384,128},{1,257},{129,385},{257,1},{385... | collective-permute-start | bytes 1966088 | tf_op jit(solution)/shard_map/ppermute | solution.py:29
  56.6 0.4 own_cols.1
  57.0 1.2 shard_map.69
  58.2 0.0 collective-permute-done.6.refs_0_
  58.2 2.3 %shard_map.70 = (f32[8,32,128]{2,1,0:T(8,128)S(1)}, bf16[2,1024,512]{2,1,0:T(8,128)(2,1)S(1)}, bf16[2,1024,512]{2,1,0:T(8,128)(2,1)S(1)}, bf16[2,512,512]{2,1,0:T(8,128)(2,1)S(1)}, f32[2,1,512]{2,1,0:T(1,128)S(1)}) custom-call(f32[8,128,128]{2,1,0:T(8,128)S(1)} %collective-permute-done.6.refs_0_, ...), custom_call_target="tpu_custom_call" | custom-call | flops 1610612736 | bytes 4194304 | tf_op jit(solution)/shard_map/pallas_call | solution.py:194
  60.5 1.2 shard_map.68
  61.7 2.3 %collective-permute-done.8.cols = f32[8,160,128]{2,1,0:T(8,128)S(1)} collective-permute-done((f32[8,160,128]{2,1,0:T(8,128)S(1)}, f32[8,160,128]{2,1,0:T(8,128)S(1)}, u32[]{:S(2)}, u32[]{:S(2)}) %collective-permute-start.8) | collective-permute-done | bytes 655392 | tf_op jit(solution)/shard_map/ppermute | solution.py:29
  64.0 4.5 %shard_map.71 = (f32[16,32,128]{2,1,0:T(8,128)S(1)}, bf16[4,1024,512]{2,1,0:T(8,128)(2,1)S(1)}, bf16[4,1024,512]{2,1,0:T(8,128)(2,1)S(1)}) custom-call(f32[8,160,128]{2,1,0:T(8,128)S(1)} %collective-permute-done.8.cols, bf16[1,512,512]{2,1,0:T(8,128)(2,1)S(1)} %get-tuple-element.45.refs_0_, bf16[1,512,512]{2,1,0:T(8,128)(2,1)S(1)} %get-tuple-element.46.refs_1_, ...), custom_call_target="tpu_custom_call" | custom-call | flops 3221225472 | bytes 8388608 | tf_op jit(solution)/shard_map/pallas_call | solution.py:205
  68.5 0.0 collective-permute-done.7.cols
  68.5 4.6 %shard_map.72 = (f32[16,32,128]{2,1,0:T(8,128)S(1)}, bf16[4,1024,512]{2,1,0:T(8,128)(2,1)S(1)}, bf16[4,1024,512]{2,1,0:T(8,128)(2,1)S(1)}) custom-call(f32[8,160,128]{2,1,0:T(8,128)S(1)} %collective-permute-done.7.cols, bf16[1,512,512]{2,1,0:T(8,128)(2,1)S(1)} %get-tuple-element.45.refs_0_, bf16[1,512,512]{2,1,0:T(8,128)(2,1)S(1)} %get-tuple-element.46.refs_1_, ...), custom_call_target="tpu_custom_call" | custom-call | flops 3221225472 | bytes 8388608 | tf_op jit(solution)/shard_map/pallas_call | solution.py:205
  73.1 6.0 %collective-permute-done.cols = f32[8,160,128]{2,1,0:T(8,128)S(1)} collective-permute-done((f32[8,160,128]{2,1,0:T(8,128)S(1)}, f32[8,160,128]{2,1,0:T(8,128)S(1)}, u32[]{:S(2)}, u32[]{:S(2)}) %collective-permute-start) | collective-permute-done | bytes 655392 | tf_op jit(solution)/shard_map/ppermute | solution.py:29
  79.1 2.6 %shard_map.74 = (f32[8,32,128]{2,1,0:T(8,128)S(1)}, bf16[2,1024,512]{2,1,0:T(8,128)(2,1)S(1)}, bf16[2,1024,512]{2,1,0:T(8,128)(2,1)S(1)}) custom-call(f32[8,160,128]{2,1,0:T(8,128)S(1)} %collective-permute-done.cols, bf16[1,512,512]{2,1,0:T(8,128)(2,1)S(1)} %get-tuple-element.45.refs_0_, bf16[1,512,512]{2,1,0:T(8,128)(2,1)S(1)} %get-tuple-element.46.refs_1_, ...), custom_call_target="tpu_custom_call" | custom-call | flops 1610612736 | bytes 4194304 | tf_op jit(solution)/shard_map/pallas_call | solution.py:205
  81.7 0.0 copy-start
  81.7 9.6 %collective-permute-start.9 = (f32[8,32,128]{2,1,0:T(8,128)S(1)}, f32[8,32,128]{2,1,0:T(8,128)S(1)}, u32[]{:S(2)}, u32[]{:S(2)}) collective-permute-start(f32[8,32,128]{2,1,0:T(8,128)S(1)} %get-tuple-element.57), channel_id=1, source_target_pairs={{0,8},{8,0},{1,9},{9,1},{2,10},{10,2},{3,11},{11,3},{4,12},{12,4},... | collective-permute-start | bytes 393224 | tf_op jit(solution)/shard_map/ppermute | solution.py:29
  91.3 2.4 %shard_map.73 = (f32[8,32,128]{2,1,0:T(8,128)S(1)}, bf16[2,1024,512]{2,1,0:T(8,128)(2,1)S(1)}, bf16[2,1024,512]{2,1,0:T(8,128)(2,1)S(1)}) custom-call(f32[8,160,128]{2,1,0:T(8,128)S(1)} %collective-permute-done.cols, bf16[1,512,512]{2,1,0:T(8,128)(2,1)S(1)} %get-tuple-element.45.refs_0_, bf16[1,512,512]{2,1,0:T(8,128)(2,1)S(1)} %get-tuple-element.46.refs_1_, ...), custom_call_target="tpu_custom_call" | custom-call | flops 1610612736 | bytes 4194304 | tf_op jit(solution)/shard_map/pallas_call | solution.py:205
  93.8 0.0 collective-permute-done.9
  93.8 14.0 %all_to_all.30.arrived = f32[8,32,128]{2,1,0:T(8,128)S(1)} all-to-all(f32[8,32,128]{2,1,0:T(8,128)S(1)} %add.6), channel_id=1, replica_groups=mesh['x'=4,'y'=8,'c'=2,'z'=8] {'z'}, dimensions={0} | all-to-all | bytes 262144 | tf_op jit(solution)/shard_map/all_to_all | solution.py:33
  107.8 0.0 copy-done
  107.8 0.1 between.1
  107.8 22.2 %all_to_all.31.gathered = f32[32,32,128]{2,1,0:T(8,128)S(1)} all-to-all(f32[32,32,128]{2,1,0:T(8,128)S(1)} %get-tuple-element.58), channel_id=1, replica_groups=mesh['x'=4,'y'=8,'c'=2,'z'=8] {'x','y'}, dimensions={0} | all-to-all | bytes 1048576 | tf_op jit(solution)/shard_map/all_to_all | solution.py:33
  130.0 3.0 %shard_map.76 = f32[8,32,128]{2,1,0:T(8,128)S(1)} custom-call(f32[32,32,128]{2,1,0:T(8,128)S(1)} %all_to_all.31.gathered, bf16[1,1024,512]{2,1,0:T(8,128)(2,1)S(1)} %get-tuple-element.59.refs_0_, bf16[1,1024,512]{2,1,0:T(8,128)(2,1)S(1)} %get-tuple-element.60.refs_1_, bf16[2,1024,512]{2,1,0:T(8,128)(2,1)S(1)} %get-tuple-element.61.refs_2_, ...), custom_call_target="tpu_custom_call" | custom-call | flops 1073741824 | bytes 16777216 | tf_op jit(solution)/shard_map/pallas_call | solution.py:263
  133.0 7.3 %collective-permute-start.10 = (f32[8,32,128]{2,1,0:T(8,128)S(1)}, f32[8,32,128]{2,1,0:T(8,128)S(1)}, u32[]{:S(2)}, u32[]{:S(2)}) collective-permute-start(f32[8,32,128]{2,1,0:T(8,128)S(1)} %shard_map.76), channel_id=1, source_target_pairs={{0,8},{8,0},{1,9},{9,1},{2,10},{10,2},{3,11},{11,3},{4,12},{12,4},... | collective-permute-start | bytes 393224 | tf_op jit(solution)/shard_map/ppermute | solution.py:29
  140.3 3.0 %shard_map.75 = f32[8,32,128]{2,1,0:T(8,128)S(1)} custom-call(f32[32,32,128]{2,1,0:T(8,128)S(1)} %all_to_all.31.gathered, bf16[1,1024,512]{2,1,0:T(8,128)(2,1)S(1)} %get-tuple-element.59.refs_0_, bf16[1,1024,512]{2,1,0:T(8,128)(2,1)S(1)} %get-tuple-element.60.refs_1_, bf16[2,1024,512]{2,1,0:T(8,128)(2,1)S(1)} %get-tuple-element.61.refs_2_, ...), custom_call_target="tpu_custom_call" | custom-call | flops 1073741824 | bytes 16777216 | tf_op jit(solution)/shard_map/pallas_call | solution.py:263
  143.3 0.0 collective-permute-done.10
  143.4 11.9 %all_to_all.32.arrived = f32[8,32,128]{2,1,0:T(8,128)S(1)} all-to-all(f32[8,32,128]{2,1,0:T(8,128)S(1)} %add.7), channel_id=1, replica_groups=mesh['x'=4,'y'=8,'c'=2,'z'=8] {'z'}, dimensions={0} | all-to-all | bytes 262144 | tf_op jit(solution)/shard_map/all_to_all | solution.py:33
  155.2 0.2 settle.1
  155.5 11.3 %all_to_all.33 = f32[16,1,128]{2,1,0:T(1,128)S(1)} all-to-all(f32[16,1,128]{2,1,0:T(1,128)S(1)} %broadcast_in_dim.19), channel_id=1, replica_groups=mesh['x'=4,'y'=8,'c'=2,'z'=8] {'y','c'}, dimensions={0} | all-to-all | bytes 16384 | tf_op jit(solution)/shard_map/all_to_all | solution.py:33
  166.9 11.6 %all_to_all.34.sums = f32[32,1,128]{2,1,0:T(1,128)S(1)} all-to-all(f32[32,1,128]{2,1,0:T(1,128)S(1)} %broadcast_in_dim.20), channel_id=1, replica_groups=mesh['x'=4,'y'=8,'c'=2,'z'=8] {'x','z'}, dimensions={0} | all-to-all | bytes 32768 | tf_op jit(solution)/shard_map/all_to_all | solution.py:33
  178.5 1.0 finish.1
  (13 shorter events, 0.2 us)
Async XLA Ops:
  3.8 29.9 %collective-permute-start.3 = (f32[128,128]{1,0:T(8,128)S(1)}, f32[128,128]{1,0:T(8,128)S(1)}, u32[]{:S(2)}, u32[]{:S(2)}) collective-permute-start(f32[128,128]{1,0:T(8,128)S(1)} %get-tuple-element.41.refs_0_), channel_id=1, source_target_pairs={{0,4},{1,5},{2,6},{3,7},{4,0},{5,1},{6,2},{7,3},{8,12},{9,13},{10,... | collective-permute-start | bytes 196616 | tf_op jit(solution)/shard_map/ppermute | solution.py:29
  15.3 12.1 %collective-permute-start.2 = (f32[128,128]{1,0:T(8,128)S(1)}, f32[128,128]{1,0:T(8,128)S(1)}, u32[]{:S(2)}, u32[]{:S(2)}) collective-permute-start(f32[128,128]{1,0:T(8,128)S(1)} %get-tuple-element.41.refs_0_), channel_id=1, source_target_pairs={{0,7},{1,0},{2,1},{3,2},{4,3},{5,4},{6,5},{7,6},{8,15},{9,8},{10,9... | collective-permute-start | bytes 196616 | tf_op jit(solution)/shard_map/ppermute | solution.py:29
  17.2 10.2 %collective-permute-start.1 = (f32[128,128]{1,0:T(8,128)S(1)}, f32[128,128]{1,0:T(8,128)S(1)}, u32[]{:S(2)}, u32[]{:S(2)}) collective-permute-start(f32[128,128]{1,0:T(8,128)S(1)} %get-tuple-element.41.refs_0_), channel_id=1, source_target_pairs={{0,1},{1,2},{2,3},{3,4},{4,5},{5,6},{6,7},{7,0},{8,9},{9,10},{10,1... | collective-permute-start | bytes 196616 | tf_op jit(solution)/shard_map/ppermute | solution.py:29
  20.6 26.1 %all-to-all-start = ((f32[8,160,128]{2,1,0:T(8,128)}), f32[8,160,128]{2,1,0:T(8,128)S(1)}, u32[]{:S(2)}, u32[]{:S(2)}) async-start(f32[8,160,128]{2,1,0:T(8,128)} %get-tuple-element.40), calls=%async_computation | async-start | bytes 1310720 | tf_op jit(solution)/shard_map/all_to_all | solution.py:33
  27.4 10.7 %collective-permute-start.5 = (f32[2,128,128]{2,1,0:T(8,128)S(1)}, f32[2,128,128]{2,1,0:T(8,128)S(1)}, u32[]{:S(2)}, u32[]{:S(2)}) collective-permute-start(f32[2,128,128]{2,1,0:T(8,128)S(1)} %get-tuple-element.76), channel_id=1, source_target_pairs={{0,6},{1,7},{2,0},{3,1},{4,2},{5,3},{6,4},{7,5},{8,14},{9,15},{10,... | collective-permute-start | bytes 393224 | tf_op jit(solution)/shard_map/ppermute | solution.py:29
  29.4 8.8 %collective-permute-start.4 = (f32[2,128,128]{2,1,0:T(8,128)S(1)}, f32[2,128,128]{2,1,0:T(8,128)S(1)}, u32[]{:S(2)}, u32[]{:S(2)}) collective-permute-start(f32[2,128,128]{2,1,0:T(8,128)S(1)} %get-tuple-element.77), channel_id=1, source_target_pairs={{0,2},{1,3},{2,4},{3,5},{4,6},{5,7},{6,0},{7,1},{8,10},{9,11},{10,... | collective-permute-start | bytes 393224 | tf_op jit(solution)/shard_map/ppermute | solution.py:29
  38.2 20.0 %collective-permute-start.6 = (f32[8,128,128]{2,1,0:T(8,128)S(1)}, f32[8,128,128]{2,1,0:T(8,128)S(1)}, u32[]{:S(2)}, u32[]{:S(2)}) collective-permute-start(f32[8,128,128]{2,1,0:T(8,128)S(1)} %constant_dynamic-update-slice_fusion), channel_id=1, source_target_pairs={{0,8},{8,0},{1,9},{9,1},{2,10},{10,2},{3,11},{11,3},{4,12},{12,4},... | collective-permute-start | bytes 1572872 | tf_op jit(solution)/shard_map/ppermute | solution.py:29
  46.6 17.4 %collective-permute-start.8 = (f32[8,160,128]{2,1,0:T(8,128)S(1)}, f32[8,160,128]{2,1,0:T(8,128)S(1)}, u32[]{:S(2)}, u32[]{:S(2)}) collective-permute-start(f32[8,160,128]{2,1,0:T(8,128)S(1)} %all-to-all-done.cols), channel_id=1, source_target_pairs={{0,128},{128,256},{256,384},{384,0},{1,129},{129,257},{257,385},{3... | collective-permute-start | bytes 1966088 | tf_op jit(solution)/shard_map/ppermute | solution.py:29
  49.8 18.7 %collective-permute-start.7 = (f32[8,160,128]{2,1,0:T(8,128)S(1)}, f32[8,160,128]{2,1,0:T(8,128)S(1)}, u32[]{:S(2)}, u32[]{:S(2)}) collective-permute-start(f32[8,160,128]{2,1,0:T(8,128)S(1)} %all-to-all-done.cols), channel_id=1, source_target_pairs={{0,384},{128,0},{256,128},{384,256},{1,385},{129,1},{257,129},{385... | collective-permute-start | bytes 1966088 | tf_op jit(solution)/shard_map/ppermute | solution.py:29
  53.1 25.9 %collective-permute-start = (f32[8,160,128]{2,1,0:T(8,128)S(1)}, f32[8,160,128]{2,1,0:T(8,128)S(1)}, u32[]{:S(2)}, u32[]{:S(2)}) collective-permute-start(f32[8,160,128]{2,1,0:T(8,128)S(1)} %all-to-all-done.cols), channel_id=1, source_target_pairs={{0,256},{128,384},{256,0},{384,128},{1,257},{129,385},{257,1},{385... | collective-permute-start | bytes 1966088 | tf_op jit(solution)/shard_map/ppermute | solution.py:29
  81.7 26.1 %copy-start = (f32[32,128]{1,0:T(8,128)S(1)}, f32[32,128]{1,0:T(8,128)}, u32[]{:S(2)}) copy-start(f32[32,128]{1,0:T(8,128)} %targets.5) | copy-start | bytes 49156
  81.7 12.1 %collective-permute-start.9 = (f32[8,32,128]{2,1,0:T(8,128)S(1)}, f32[8,32,128]{2,1,0:T(8,128)S(1)}, u32[]{:S(2)}, u32[]{:S(2)}) collective-permute-start(f32[8,32,128]{2,1,0:T(8,128)S(1)} %get-tuple-element.57), channel_id=1, source_target_pairs={{0,8},{8,0},{1,9},{9,1},{2,10},{10,2},{3,11},{11,3},{4,12},{12,4},... | collective-permute-start | bytes 393224 | tf_op jit(solution)/shard_map/ppermute | solution.py:29
  133.0 10.3 %collective-permute-start.10 = (f32[8,32,128]{2,1,0:T(8,128)S(1)}, f32[8,32,128]{2,1,0:T(8,128)S(1)}, u32[]{:S(2)}, u32[]{:S(2)}) collective-permute-start(f32[8,32,128]{2,1,0:T(8,128)S(1)} %shard_map.76), channel_id=1, source_target_pairs={{0,8},{8,0},{1,9},{9,1},{2,10},{10,2},{3,11},{11,3},{4,12},{12,4},... | collective-permute-start | bytes 393224 | tf_op jit(solution)/shard_map/ppermute | solution.py:29
